TPU v7x, 32 devices: a whole 2x2x4 slice. The times are simulated.
32 devices in a mesh: grp: 4 (over z), dev: 8 (over y, x, core).
Axes of the slice: x: 2, y: 2, z: 4, core: 2. Of those that a mesh axis runs over, the one named last changes fastest.
Arguments:
- atoms: bfloat16 [8192, 768], P(('grp', 'dev')), may hold values from -6 to 6
- positions: float32 [3, 8192], P(None, ('grp', 'dev')), may hold values from -6 to 6
- segment: int32 [8192], P(('grp', 'dev')), may hold values from 0 to 8191, as said below
- item_time: float32 [8192], P(('grp', 'dev')), may hold values from 0 to 1, as said below
- time_weight: bfloat16 [128, 768], P(None, ('grp', 'dev')), may hold values from -0.5 to 0.5
- norm1_gain: bfloat16 [768], P(('grp', 'dev')), may hold values from 0.5 to 1.5
- norm1_bias: bfloat16 [768], P(('grp', 'dev')), may hold values from -3 to 3
- qkv_weight: bfloat16 [768, 2304], P(('grp', 'dev')), may hold values from -0.21875 to 0.21875
- out_weight: bfloat16 [768, 768], P(('grp', 'dev')), may hold values from -1.75 to 1.75
- norm2_gain: bfloat16 [768], P(('grp', 'dev')), may hold values from 0.5 to 1.5
- norm2_bias: bfloat16 [768], P(('grp', 'dev')), may hold values from -3 to 3
- ffn_in: bfloat16 [768, 3072], P(('grp', 'dev')), may hold values from -0.21875 to 0.21875
- ffn_in_bias: bfloat16 [3072], P(('grp', 'dev')), may hold values from -3 to 3
- ffn_out: bfloat16 [3072, 768], P(('grp', 'dev')), may hold values from -0.109375 to 0.109375
- ffn_out_bias: bfloat16 [768], P(('grp', 'dev')), may hold values from -3 to 3
- pair_weight: bfloat16 [128, 32], replicated, may hold values from -4 to 4
- kernel_mean: float32 [128], replicated, may hold values from 0 to 12
- kernel_width: float32 [128], replicated, may hold values from 0.5 to 3
- cotangent: bfloat16 [8192, 768], P(('grp', 'dev')), may hold values from -6 to 6
Outputs:
- output: bfloat16 [8192, 768], P(('grp', 'dev'))
- grad_atoms: float32 [8192, 768], P(('grp', 'dev'))
- grad_time_weight: float32 [128, 768], P(None, ('grp', 'dev'))
- grad_norm1_gain: float32 [768], P(('grp', 'dev'))
- grad_norm1_bias: float32 [768], P(('grp', 'dev'))
- grad_qkv_weight: float32 [768, 2304], P(('grp', 'dev'))
- grad_out_weight: float32 [768, 768], P(('grp', 'dev'))
- grad_norm2_gain: float32 [768], P(('grp', 'dev'))
- grad_norm2_bias: float32 [768], P(('grp', 'dev'))
- grad_ffn_in: float32 [768, 3072], P(('grp', 'dev'))
- grad_ffn_in_bias: float32 [3072], P(('grp', 'dev'))
- grad_ffn_out: float32 [3072, 768], P(('grp', 'dev'))
- grad_ffn_out_bias: float32 [768], P(('grp', 'dev'))
- grad_pair_weight: float32 [128, 32], replicated
- grad_kernel_mean: float32 [128], replicated
- grad_kernel_width: float32 [128], replicated
Inputs may be any that keep to these rules, and one draw needn't show every extreme that they name: `segment`: an atom's item number is the index of the last atom of its item; numbers never fall along the atoms; each item is a run of equal numbers inside one aligned block of 1024 atoms and holds 1 to 1024 atoms; in every draw some block is one item of 1024 atoms. `item_time`: equal for all atoms of one item.
All inputs are finite; a program needn't handle non-finite values.
Results may differ from a plain program's by a relative error of at most 0.012.
The roundings to bfloat16 on the way count: a program that leaves them out, or rounds other values in their place, can miss the bound.
Values may be sent and summed in bfloat16 or wider, within the bound.
A program may use at most 256 MiB of HBM per device.

v0:
```python
from functools import partial
import itertools
import math

import jax
import jax.numpy as jnp
from jax import lax
from jax.experimental import pallas as pl
from jax.experimental.pallas import tpu as pltpu
from jax.sharding import PartitionSpec as P
import ml_dtypes
import numpy as np

D = 768
HEADS = 32
HDIM = 24
KERN = 128
TFREQ = 128
BIN = 1024
GROUPS = 4
GHEADS = HEADS // GROUPS
GWIDTH = GHEADS * HDIM
PAIR_ROWS = 16
GRAD_ROWS = 32
ATT_ROWS = 128
UNIT_LANES = 768
UNIT_ROWS = 32
FEED_LANES = 512
SLACK = 2
LAST_TURNS = 5
VECTORS = 6

norm_eps = 1e-05
mask_fill = -1e30
log2e = math.log2(math.e)
center = 6.0
f32 = jnp.float32
bf16 = jnp.bfloat16
VMEM_LIMIT = 58 * 1024 * 1024
MESH = pl.DeviceIdType.MESH


def dot(left, right):
    return jnp.dot(left, right, preferred_element_type=f32)


def lanes_dot(left, right):
    return lax.dot_general(left, right, (((1,), (1,)), ((), ())), preferred_element_type=f32)


def rows_dot(left, right):
    return lax.dot_general(left, right, (((0,), (0,)), ((), ())), preferred_element_type=f32)


def grid_of_mesh(mesh):
    count = mesh.shape["dev"] // 2
    wide = 1
    while wide * wide < count:
        wide *= 2
    return mesh.shape["grp"], count // wide, wide, 2


def my_place(sizes):
    _, _, wide, cores = sizes
    dev = lax.axis_index("dev")
    return (lax.axis_index("grp"), dev // (wide * cores), lax.rem(dev // cores, wide), lax.rem(dev, cores))


def device_at(place, sizes):
    _, _, wide, cores = sizes
    return (place[0], (place[1] * wide + place[2]) * cores + place[3])


def other_place(place, axis, shift, sizes):
    moved = list(place)
    moved[axis] = lax.rem(place[axis] + shift, sizes[axis])
    return tuple(moved)


def block_partners(place):
    _, _, x, core = place
    beside, across = 1 - core, x + 1 - 2 * lax.rem(x, 2)
    return (
        place[:3] + (beside,),
        place[:2] + (across, core),
        place[:2] + (across, beside),
    )


def axis_partners(place, sizes):
    return [other_place(place, axis, shift, sizes) for axis in range(4) for shift in range(1, sizes[axis])]


def meet(partners, sizes):
    barrier = pltpu.get_barrier_semaphore()
    for partner in partners:
        pl.semaphore_signal(barrier, inc=1, device_id=device_at(partner, sizes), device_id_type=MESH)
    pl.semaphore_wait(barrier, len(partners))


def send(source, goal, sems, at, partner, sizes):
    return pltpu.make_async_remote_copy(
        src_ref=source,
        dst_ref=goal,
        send_sem=sems[0].at[at],
        recv_sem=sems[1].at[at],
        device_id=device_at(partner, sizes),
        device_id_type=MESH,
    )


class Staged:
    def place_stages(self, order, place, sizes):
        self.order, self.place, self.sizes = order, place, sizes
        self.base = [0]
        for axis in order:
            self.base.append(self.base[-1] + sizes[axis] - 1)

    def copies(self, stage):
        found = []
        for shift in range(1, self.sizes[self.order[stage]]):
            target = other_place(self.place, self.order[stage], shift, self.sizes)
            source, goal = self.ends(stage, shift, target)
            sem = self.base[stage] + shift - 1
            found.append(
                pltpu.make_async_remote_copy(
                    src_ref=source,
                    dst_ref=goal,
                    send_sem=self.send_sem.at[self.at, sem],
                    recv_sem=self.recv_sem.at[self.at, sem],
                    device_id=device_at(target, self.sizes),
                    device_id_type=MESH,
                )
            )
        return found

    def start(self, stage):
        for copy in self.copies(stage):
            copy.start()

    def arrive(self, stage):
        for copy in self.copies(stage):
            copy.wait_recv()

    def finish(self):
        for stage in range(len(self.order)):
            for copy in self.copies(stage):
                copy.wait_send()


class GatherPart(Staged):
    def __init__(self, source, full, rows, lanes, order, at, send_sem, recv_sem, place, sizes):
        self.source, self.full, self.rows, self.lanes = source, full, rows, lanes
        self.at, self.send_sem, self.recv_sem = at, send_sem, recv_sem
        self.place_stages(order, place, sizes)

    def ends(self, stage, shift, target):
        done = self.order[:stage]
        where = tuple(slice(None) if axis in done else self.place[axis] for axis in range(4))
        held = self.full.at[where + (self.rows, self.lanes)]
        return (self.source.at[self.rows, self.lanes] if stage == 0 else held), held


class ScatterPart(Staged):
    def __init__(self, source, result, rows, lanes, order, buffers, at, send_sem, recv_sem, own_sem, place, sizes):
        self.source, self.result, self.rows, self.lanes = source, result, rows, lanes
        self.first, self.slots = buffers[0], buffers[1:]
        self.at, self.send_sem, self.recv_sem, self.own_sem = at, send_sem, recv_sem, own_sem
        self.place_stages(order, place, sizes)

    def pick(self, stage, index):
        if stage == 0:
            where = tuple(index if axis == self.order[0] else slice(None) for axis in range(4))
            return self.source.at[where + (self.rows, self.lanes)]
        holder = self.first if stage == 1 else self.slots[stage - 1].at[0]
        left = [axis for axis in range(4) if axis not in self.order[:stage]]
        return holder.at[tuple(index if axis == self.order[stage] else slice(None) for axis in left)]

    def own_copy(self):
        return pltpu.make_async_copy(self.pick(0, self.place[self.order[0]]), self.first, self.own_sem.at[self.at])

    def ends(self, stage, shift, target):
        return self.pick(stage, target[self.order[stage]]), self.slots[stage].at[shift - 1]

    def start(self, stage):
        if stage == 0:
            self.own_copy().start()
        super().start(stage)

    def arrive(self, stage):
        if stage == 0:
            self.own_copy().wait()
        super().arrive(stage)
        slots = self.slots[stage]
        count = self.sizes[self.order[stage]] - 1
        mine = self.first if stage == 0 else self.pick(stage, self.place[self.order[stage]])
        lead = slots.shape[1:-2]
        if not lead:
            total = mine[...].astype(f32)
            for slot in range(count):
                total = total + slots[slot].astype(f32)
            self.result[self.rows, self.lanes] = total
            return

        def add(outer, carry):
            for inner in itertools.product(*map(range, lead[1:])):
                where = (outer,) + inner
                total = mine[where].astype(f32)
                for slot in range(count):
                    total = total + slots[(slot,) + where].astype(f32)
                if stage == 0:
                    self.first[where] = total.astype(bf16)
                else:
                    slots[(0,) + where] = total.astype(bf16)
            return carry

        lax.fori_loop(0, lead[0], add, 0)


class TotalPart(Staged):
    def __init__(self, source, result, slots, send_sem, recv_sem, place, sizes):
        self.source, self.result, self.slots = source, result, slots
        self.at, self.send_sem, self.recv_sem = 0, send_sem, recv_sem
        self.place_stages((3, 2, 1, 0), place, sizes)

    def ends(self, stage, shift, target):
        mine = self.slots[stage].at[self.place[self.order[stage]]]
        return mine, mine

    def start(self, stage):
        if stage == 0:
            self.slots[0][self.place[3]] = self.source[...]
        super().start(stage)

    def arrive(self, stage):
        super().arrive(stage)
        total = self.slots[stage][0]
        for at in range(1, self.sizes[self.order[stage]]):
            total = total + self.slots[stage][at]
        if stage == 3:
            self.result[...] = total
        else:
            self.slots[stage + 1][self.place[self.order[stage + 1]]] = total


def stage_turns(groups, stages=4, slack=SLACK):
    def opening():
        for group in groups[:slack]:
            for part in group:
                part.start(0)

    def turn(at):
        if at + slack < len(groups):
            for part in groups[at + slack]:
                part.start(0)
        for stage in range(stages - 1, -1, -1):
            index = at - slack * stage
            if 0 <= index < len(groups):
                for part in groups[index]:
                    part.arrive(stage)
                    if stage + 1 < stages:
                        part.start(stage + 1)

    def closing():
        for group in groups:
            for part in group:
                part.finish()

    return opening, [partial(turn, at) for at in range(len(groups) + slack * (stages - 1))], closing


def spread_turns(step, steps, turns, phase=0, phases=1):
    span = steps * phases - 1
    for at in range(steps):
        point = at * phases + phase - 1
        todo = turns[point * len(turns) // span : (point + 1) * len(turns) // span] if point >= 0 else []
        if todo:

            @pl.when(step == at)
            def _():
                for turn in todo:
                    turn()


def pieces(rows, lanes):
    if rows > UNIT_ROWS and rows % UNIT_ROWS == 0:
        return [(at, UNIT_ROWS, 0, lanes) for at in range(0, rows, UNIT_ROWS)]
    if lanes > UNIT_LANES and lanes % UNIT_LANES == 0:
        return [(0, rows, at, UNIT_LANES) for at in range(0, lanes, UNIT_LANES)]
    return [(0, rows, 0, lanes)]


def make_plan(shapes, first_order, second_order):
    plan = []
    for at, (rows, lanes) in enumerate(shapes):
        for row, height, lane, width in pieces(rows, lanes):
            half = width // 256 * 128
            group = [(at, (row, height), (lane + half, width - half), second_order)]
            if half:
                group.insert(0, (at, (row, height), (lane, half), first_order))
            plan.append(group)
    return plan


def part_count(plan):
    return sum(map(len, plan))


def slot_count(sizes):
    return sum(size - 1 for size in sizes)


def gather_plan(shapes):
    return make_plan(shapes, (0, 2, 1, 3), (0, 1, 2, 3))


def gather_groups(plan, sources, fulls, send_sem, recv_sem, place, sizes):
    groups, index = [], 0
    for group in plan:
        groups.append([])
        for at, rows, lanes, order in group:
            groups[-1].append(
                GatherPart(
                    sources[at], fulls[at], pl.ds(*rows), pl.ds(*lanes), order, index, send_sem, recv_sem, place, sizes
                )
            )
            index += 1
    return groups


def scatter_plan(shapes):
    return make_plan(shapes, (3, 2, 1, 0), (3, 1, 2, 0))


def scatter_scratch(sizes, plan):
    parts, slots = part_count(plan), slot_count(sizes)
    scratch = [
        pltpu.SemaphoreType.DMA((parts, slots)),
        pltpu.SemaphoreType.DMA((parts, slots)),
        pltpu.SemaphoreType.DMA((parts,)),
    ]
    for at, rows, lanes, order in sum(plan, []):
        block = (rows[1], lanes[1])
        left = [0, 1, 2, 3]
        for stage, axis in enumerate(order):
            left.remove(axis)
            lead = tuple(sizes[other] for other in left)
            if stage == 0:
                scratch.append(pltpu.VMEM(lead + block, bf16))
            scratch.append(pltpu.VMEM((sizes[axis] - 1,) + lead + block, bf16))
    return scratch


def scatter_groups(plan, sources, results, scratch, place, sizes):
    send_sem, recv_sem, own_sem = scratch[:3]
    groups, index = [], 0
    for group in plan:
        groups.append([])
        for at, rows, lanes, order in group:
            held = scratch[3 + 5 * index : 8 + 5 * index]
            groups[-1].append(
                ScatterPart(
                    sources[at],
                    results[at],
                    pl.ds(*rows),
                    pl.ds(*lanes),
                    order,
                    held,
                    index,
                    send_sem,
                    recv_sem,
                    own_sem,
                    place,
                    sizes,
                )
            )
            index += 1
    return groups


def scatter_shapes(sizes, arrays):
    return [(array.shape[0] // math.prod(sizes), array.shape[1]) for array in arrays]


anywhere = pl.BlockSpec(memory_space=pl.ANY)
in_vmem = pl.BlockSpec(memory_space=pltpu.VMEM)


def pair_block(places_i, keys, coef, weight_t, dist_ref, phi_ref, bias_ref, mask_scr, between):
    square = None
    for axis in range(3):
        gap = places_i[:, axis : axis + 1] - keys[axis : axis + 1, :]
        square = gap * gap if square is None else square + gap * gap
    dist_ref[...] = jnp.sqrt(square)
    mask_scr[...] = jnp.where(places_i[:, 3:4] == keys[3:4, :], 0.0, mask_fill).astype(f32)
    for u in range(PAIR_ROWS):
        if u == PAIR_ROWS // 2:
            between()
        for kg in range(KERN // 16):
            rows = slice(kg * 16, kg * 16 + 16)
            mean, inv, shift = coef[0, rows, :], coef[1, rows, :], coef[2, rows, :]
            for jv in range(BIN // 128):
                z = (dist_ref[u : u + 1, jv * 128 : jv * 128 + 128] - mean) * inv
                lanes = slice(u * BIN + jv * 128, u * BIN + jv * 128 + 128)
                phi_ref[rows, lanes] = jnp.exp2(shift - z * z).astype(bf16)
    bias = dot(weight_t[...], phi_ref[...])
    for u in range(PAIR_ROWS):
        part = bias[:, u * BIN : u * BIN + BIN] * log2e + mask_scr[u : u + 1, :]
        for g in range(GROUPS):
            bias_ref[g, u * GHEADS : u * GHEADS + GHEADS, :] = part[g * GHEADS : g * GHEADS + GHEADS, :]


def pair_kernel(sizes, plan, count, steps, positions, items, mean, width, weight_t, time_weight, *refs):
    vectors, refs = refs[:VECTORS], refs[VECTORS:]
    sources, refs = (refs[-1],) + refs[: count - 1], refs[count - 1 : -1]
    (dist_ref, phi_ref, bias_ref), refs = refs[:3], refs[3:]
    fulls, refs = refs[:count], refs[count:]
    mask_scr, keys, columns, coef, send_sem, recv_sem, own_sem, place_send, place_recv = refs
    step = pl.program_id(0)
    place = my_place(sizes)
    rows = positions.shape[1]
    opening, turns, closing = stage_turns(gather_groups(plan, sources, fulls, send_sem, recv_sem, place, sizes))
    own = [pltpu.make_async_copy(sources[at], fulls[at].at[place], own_sem.at[at]) for at in range(count)]
    shared = [
        send(
            keys.at[:, pl.ds(0, rows)],
            keys.at[:, pl.ds((at + 1) * rows, rows)],
            (place_send, place_recv),
            at,
            partner,
            sizes,
        )
        for at, partner in enumerate(block_partners(place))
    ]

    @pl.when(step == 0)
    def _():
        here = jnp.concatenate([positions[...], items[...], jnp.zeros((4, rows), f32)], axis=0)
        keys[:, pl.ds(0, rows)] = here
        columns[...] = here.T
        square = lambda values: jnp.broadcast_to(values, (KERN, KERN)).T
        coef[0] = square(mean[...])
        coef[1] = square(math.sqrt(0.5 * log2e) / width[...])
        coef[2] = square(-log2e * jnp.log(math.sqrt(2.0 * math.pi) * width[...]))
        mask_scr[...] = jnp.zeros_like(mask_scr)
        for at, vector in enumerate(vectors):
            mask_scr[at : at + 1, pl.ds(0, vector.shape[1])] = vector[...].astype(f32)
        rest = mask_scr[0 : sources[0].shape[0] - time_weight.shape[1], pl.ds(0, TFREQ)]
        sources[0][...] = jnp.concatenate([time_weight[...].astype(f32).T, rest], axis=0).astype(bf16)
        meet(axis_partners(place, sizes) + [block_partners(place)[2]], sizes)
        for copy in own:
            copy.start()
        for copy in shared:
            copy.start()
        opening()
        for copy in own:
            copy.wait()
        for copy in shared:
            copy.wait()

    spread_turns(step, steps, turns, 0, 2)
    pair_block(
        columns[pl.ds(pl.multiple_of(step * PAIR_ROWS, PAIR_ROWS), PAIR_ROWS), :],
        keys,
        coef,
        weight_t,
        dist_ref,
        phi_ref.at[0],
        bias_ref,
        mask_scr,
        lambda: spread_turns(step, steps, turns, 1, 2),
    )

    @pl.when(step == steps - 1)
    def _():
        closing()


def pair_call(sizes, positions, items, mean, width, weight_t, time_weight, vectors, arrays, collective):
    rows = positions.shape[1]
    count = 1 + len(arrays)
    steps = rows // PAIR_ROWS
    own = time_weight.shape[1]
    small = jax.ShapeDtypeStruct((own + 8, TFREQ), bf16)
    plan = gather_plan([array.shape for array in (small, *arrays)])
    parts, slots = part_count(plan), slot_count(sizes)
    outs = pl.pallas_call(
        partial(pair_kernel, sizes, plan, count, steps),
        grid=(steps,),
        in_specs=[in_vmem] * (6 + VECTORS) + [anywhere] * len(arrays),
        out_specs=[
            pl.BlockSpec((PAIR_ROWS, BIN), lambda i: (i, 0)),
            pl.BlockSpec((1, KERN, PAIR_ROWS * BIN), lambda i: (i, 0, 0)),
            pl.BlockSpec((GROUPS, PAIR_ROWS * GHEADS, BIN), lambda i: (0, i, 0)),
        ]
        + [anywhere] * count,
        out_shape=[
            jax.ShapeDtypeStruct((rows, BIN), f32),
            jax.ShapeDtypeStruct((steps, KERN, PAIR_ROWS * BIN), bf16),
            jax.ShapeDtypeStruct((GROUPS, rows * GHEADS, BIN), f32),
        ]
        + [jax.ShapeDtypeStruct(sizes + array.shape, array.dtype) for array in (small, *arrays)],
        scratch_shapes=[
            pltpu.VMEM((PAIR_ROWS, BIN), f32),
            pltpu.VMEM((8, BIN), f32),
            pltpu.VMEM((rows, 8), f32),
            pltpu.VMEM((3, KERN, KERN), f32),
            pltpu.SemaphoreType.DMA((parts, slots)),
            pltpu.SemaphoreType.DMA((parts, slots)),
            pltpu.SemaphoreType.DMA((count,)),
            pltpu.SemaphoreType.DMA((3,)),
            pltpu.SemaphoreType.DMA((3,)),
            pltpu.VMEM(small.shape, bf16),
        ],
        compiler_params=pltpu.CompilerParams(
            collective_id=collective, has_side_effects=True, vmem_limit_bytes=VMEM_LIMIT
        ),
        name="pair_bias_and_gather",
    )(positions, items, mean, width, weight_t, time_weight, *vectors, *arrays)
    return outs[0], outs[1], outs[2], [full.reshape((-1,) + full.shape[4:]) for full in outs[3:]]


def spread_tables():
    row = np.arange(ATT_ROWS * GHEADS)
    spread = row[:, None] // GHEADS == np.arange(ATT_ROWS)[None, :]
    head = row[:, None] % GHEADS == np.arange(GWIDTH)[None, :] // HDIM
    return tuple(jnp.asarray(table.astype(ml_dtypes.bfloat16)) for table in (spread, spread.T, head, head.T))


table_specs = [in_vmem] * 4


class BlockShare:
    def __init__(self, own, full, far, near, forward, place, sizes):
        self.own, self.full, self.sizes = own, full, sizes
        self.far_sems, self.near_sems, self.forward_sems = far, near, forward
        self.beside, self.across, _ = block_partners(place)
        self.width = own.shape[1]

    def rows(self, g, which):
        return pl.ds(which * D + g * GWIDTH, GWIDTH)

    def lanes(self, at):
        return pl.ds(at * self.width, self.width)

    def far(self, g):
        return [
            send(
                self.own.at[self.rows(g, which)],
                self.full.at[self.rows(g, which), self.lanes(2)],
                self.far_sems,
                g * 2 + which,
                self.across,
                self.sizes,
            )
            for which in range(2)
        ]

    def near(self, g):
        return [
            send(
                self.own.at[self.rows(g, which)],
                self.full.at[self.rows(g, which), self.lanes(1)],
                self.near_sems,
                g * 2 + which,
                self.beside,
                self.sizes,
            )
            for which in range(2)
        ]

    def forward(self, g):
        return [
            send(
                self.full.at[self.rows(g, which), self.lanes(2)],
                self.full.at[self.rows(g, which), self.lanes(3)],
                self.forward_sems,
                g * 2 + which,
                self.beside,
                self.sizes,
            )
            for which in range(2)
        ]

    def open(self):
        for copy in self.far(0) + self.far(1):
            copy.start()
        for g in range(GROUPS):
            for copy in self.near(g):
                copy.start()

    def pass_on(self, g):
        for copy in self.far(g):
            copy.wait_recv()
        for copy in self.forward(g) + (self.far(g + 2) if g + 2 < GROUPS else []):
            copy.start()

    def ready(self, g):
        for copy in self.near(g) + self.forward(g):
            copy.wait_recv()

    def close(self):
        for g in range(GROUPS):
            for copy in self.far(g) + self.near(g) + self.forward(g):
                copy.wait_send()


def forward_kernel(
    sizes, plan, count, parts, q_ref, own_ref, bias_ref, spread, gather, head, head_t, *refs
):
    sources, refs = refs[:count], refs[count:]
    (out_ref, prob_ref, kv_out), refs = refs[:3], refs[3:]
    fulls, refs = refs[:count], refs[count:]
    (kv_ref, out_sems), sems, (send_sem, recv_sem, own_sem) = refs[:2], refs[2:8], refs[8:]
    group, part = pl.program_id(0), pl.program_id(1)
    step, steps = group * parts + part, GROUPS * parts
    place = my_place(sizes)
    share = BlockShare(own_ref, kv_ref, sems[0:2], sems[2:4], sems[4:6], place, sizes)
    opening, turns, closing = stage_turns(gather_groups(plan, sources, fulls, send_sem, recv_sem, place, sizes))
    held = [pltpu.make_async_copy(sources[at], fulls[at].at[place], own_sem.at[at]) for at in range(count)]
    kept = [
        pltpu.make_async_copy(kv_ref.at[share.rows(g, which)], kv_out.at[share.rows(g, which)], out_sems.at[g * 2 + which])
        for g in range(GROUPS)
        for which in range(2)
    ]
    for g in range(GROUPS):

        @pl.when((group == g) & (part == 0))
        def _():
            if g == 0:
                kv_ref[:, pl.ds(0, share.width)] = own_ref[...]
                meet(axis_partners(place, sizes), sizes)
                share.open()
                for copy in held:
                    copy.start()
                opening()
                for copy in held:
                    copy.wait()
                share.pass_on(0)
            share.ready(g)
            for copy in kept[2 * g : 2 * g + 2]:
                copy.start()

        if g + 1 < GROUPS:

            @pl.when((group == g) & (part == parts - 1))
            def _():
                share.pass_on(g + 1)

    spread_turns(step, steps, turns, 0, 2)
    first_row = pl.multiple_of(group * GWIDTH, GWIDTH)
    key_rows, value_rows = pl.ds(first_row, GWIDTH), pl.ds(pl.multiple_of(D + first_row, GWIDTH), GWIDTH)
    wide = ATT_ROWS * GHEADS
    query = lanes_dot(spread[...], q_ref[...]).astype(bf16) * head[...]
    chunk = 256
    for first in range(0, wide, chunk):
        at = slice(first, first + chunk)
        score = dot(query[at], kv_ref[key_rows, :]) * (HDIM**-0.5 * log2e) + bias_ref[0, at, :]
        top = jnp.max(score, axis=-1, keepdims=True)
        weight = jnp.exp2(score - top)
        total = jnp.sum(weight, axis=-1, keepdims=True)
        prob_ref[0, at, :] = (weight * (1.0 / total)).astype(bf16)
    spread_turns(step, steps, turns, 1, 2)
    mixed = lanes_dot(kv_ref[value_rows, :], prob_ref[0]).astype(bf16) * head_t[...]
    out_ref[...] = lanes_dot(mixed, gather[...]).astype(bf16)

    @pl.when((group == GROUPS - 1) & (part == parts - 1))
    def _():
        closing()
        share.close()
        for copy in kept:
            copy.wait()


def forward_call(sizes, q_t, kv_t, bias, tables, arrays, collective):
    rows = q_t.shape[1]
    wide = ATT_ROWS * GHEADS
    parts = rows // ATT_ROWS
    count = len(arrays)
    plan = gather_plan([array.shape for array in arrays])
    pieces_held, slots = part_count(plan), slot_count(sizes)
    outs = pl.pallas_call(
        partial(forward_kernel, sizes, plan, count, parts),
        grid=(GROUPS, parts),
        in_specs=[
            pl.BlockSpec((GWIDTH, ATT_ROWS), lambda g, i: (g, i)),
            in_vmem,
            pl.BlockSpec((1, wide, BIN), lambda g, i: (g, i, 0)),
        ]
        + table_specs
        + [anywhere] * count,
        out_specs=[
            pl.BlockSpec((GWIDTH, ATT_ROWS), lambda g, i: (g, i)),
            pl.BlockSpec((1, wide, BIN), lambda g, i: (g, i, 0)),
            anywhere,
        ]
        + [anywhere] * count,
        out_shape=[
            jax.ShapeDtypeStruct((D, rows), bf16),
            jax.ShapeDtypeStruct((GROUPS, rows * GHEADS, BIN), bf16),
            jax.ShapeDtypeStruct((2 * D, BIN), bf16),
        ]
        + [jax.ShapeDtypeStruct(sizes + array.shape, array.dtype) for array in arrays],
        scratch_shapes=[pltpu.VMEM((2 * D, BIN), bf16)]
        + [pltpu.SemaphoreType.DMA((2 * GROUPS,))] * 7
        + [pltpu.SemaphoreType.DMA((pieces_held, slots))] * 2
        + [pltpu.SemaphoreType.DMA((count,))],
        compiler_params=pltpu.CompilerParams(
            collective_id=collective, has_side_effects=True, vmem_limit_bytes=VMEM_LIMIT
        ),
        name="attention_forward",
    )(q_t, kv_t, bias, *tables, *arrays)
    return outs[0], outs[1], outs[2], [full.reshape((-1, full.shape[-1])) for full in outs[3:]]


class BlockSum:
    def __init__(self, outbox, near, far, result, near_sems, far_sems, place, sizes):
        self.outbox, self.near, self.far, self.result = outbox, near, far, result
        self.near_sems, self.far_sems = near_sems, far_sems
        self.sizes = sizes
        self.beside, self.across, _ = block_partners(place)
        self.width = result.shape[1]

    def block(self, g, which, at):
        return self.outbox.at[g, which, :, pl.ds(at * self.width, self.width)]

    def near_copies(self, g):
        return [
            send(
                self.block(g, which, 2 * slot + 1),
                self.near.at[g, which, slot],
                self.near_sems,
                g * 4 + which * 2 + slot,
                self.beside,
                self.sizes,
            )
            for which in range(2)
            for slot in range(2)
        ]

    def far_copies(self, g):
        return [
            send(self.block(g, which, 2), self.far.at[g, which], self.far_sems, g * 2 + which, self.across, self.sizes)
            for which in range(2)
        ]

    def open(self, g):
        for copy in self.near_copies(g):
            copy.start()

    def middle(self, g):
        for copy in self.near_copies(g):
            copy.wait_recv()
        for which in range(2):
            here = self.block(g, which, 2)
            here[...] = (here[...].astype(f32) + self.near[g, which, 1].astype(f32)).astype(bf16)
        for copy in self.far_copies(g):
            copy.start()

    def close(self, g):
        for copy in self.far_copies(g):
            copy.wait_recv()
        for which in range(2):
            total = self.block(g, which, 0)[...].astype(f32) + self.near[g, which, 0].astype(f32)
            total = total + self.far[g, which].astype(f32)
            self.result[pl.ds(which * D + g * GWIDTH, GWIDTH), :] = total.astype(bf16)

    def finish(self):
        for g in range(GROUPS):
            for copy in self.near_copies(g) + self.far_copies(g):
                copy.wait_send()


def backward_kernel(
    sizes, plan, count, steps, q_ref, go_ref, k_ref, v_ref, prob_ref, spread, gather, head, head_t, *refs
):
    sources, refs = refs[:count], refs[count:]
    (gs_ref, gq_ref, own_ref), refs = refs[:3], refs[3:]
    results, refs = refs[:count], refs[count:]
    (key_sum, value_sum, outbox, near, far), refs = refs[:5], refs[5:]
    near_sems, far_sems, scratch = refs[:2], refs[2:4], refs[4:]
    group, part, parts = pl.program_id(0), pl.program_id(1), steps // GROUPS
    step = group * parts + part
    place = my_place(sizes)
    block = BlockSum(outbox, near, far, own_ref, near_sems, far_sems, place, sizes)
    if count:
        opening, turns, closing = stage_turns(scatter_groups(plan, sources, results, scratch, place, sizes))

    @pl.when(step == 0)
    def _():
        partners = axis_partners(place, sizes) if count else [block.beside, block.across]
        meet(partners, sizes)
        if count:
            opening()

    for g in range(1, GROUPS):

        @pl.when((group == g) & (part == 0))
        def _():
            block.middle(g - 1)
            if g >= 2:
                block.close(g - 2)

    if count:
        spread_turns(step, steps, turns, 0, 2)

    wide = ATT_ROWS * GHEADS
    grad_out = lanes_dot(spread[...], go_ref[...]).astype(bf16) * head[...]
    chunk = 256
    for first in range(0, wide, chunk):
        at = slice(first, first + chunk)
        prob = prob_ref[0, at, :].astype(f32)
        grad_prob = dot(grad_out[at], v_ref[...])
        inner = jnp.sum(prob * grad_prob, axis=-1, keepdims=True)
        gs_ref[0, at, :] = (prob * (grad_prob - inner)).astype(bf16)
    if count:
        spread_turns(step, steps, turns, 1, 2)

    grad_query = lanes_dot(k_ref[...], gs_ref[0]) * (HDIM**-0.5)
    gq_ref[...] = lanes_dot(grad_query.astype(bf16) * head_t[...], gather[...]).astype(bf16)
    query_t = lanes_dot(q_ref[...], spread[...]).astype(bf16) * head_t[...]
    grad_out_t = lanes_dot(go_ref[...], spread[...]).astype(bf16) * head_t[...]
    grad_key = dot(query_t, gs_ref[0])
    grad_value = dot(grad_out_t, prob_ref[0])

    @pl.when(part == 0)
    def _():
        key_sum[...] = grad_key
        value_sum[...] = grad_value

    @pl.when(part > 0)
    def _():
        key_sum[...] += grad_key
        value_sum[...] += grad_value

    for g in range(GROUPS):

        @pl.when((group == g) & (part == parts - 1))
        def _():
            outbox[g, 0] = (key_sum[...] * (HDIM**-0.5)).astype(bf16)
            outbox[g, 1] = value_sum[...].astype(bf16)
            block.open(g)

    @pl.when(step == steps - 1)
    def _():
        block.middle(GROUPS - 1)
        block.close(GROUPS - 2)
        if count:
            closing()
        block.close(GROUPS - 1)
        block.finish()


def backward_call(sizes, q_t, go_t, kv_t, prob, tables, arrays, collective):
    rows = q_t.shape[1]
    wide = ATT_ROWS * GHEADS
    parts = rows // ATT_ROWS
    count = len(arrays)
    shapes = scatter_shapes(sizes, arrays)
    plan = scatter_plan(shapes)
    return pl.pallas_call(
        partial(backward_kernel, sizes, plan, count, GROUPS * parts),
        grid=(GROUPS, parts),
        in_specs=[
            pl.BlockSpec((GWIDTH, ATT_ROWS), lambda g, i: (g, i)),
            pl.BlockSpec((GWIDTH, ATT_ROWS), lambda g, i: (g, i)),
            pl.BlockSpec((GWIDTH, BIN), lambda g, i: (g, 0)),
            pl.BlockSpec((GWIDTH, BIN), lambda g, i: (g + GROUPS, 0)),
            pl.BlockSpec((1, wide, BIN), lambda g, i: (g, i, 0)),
        ]
        + table_specs
        + [anywhere] * count,
        out_specs=[
            pl.BlockSpec((1, wide, BIN), lambda g, i: (g, i, 0)),
            pl.BlockSpec((GWIDTH, ATT_ROWS), lambda g, i: (g, i)),
            in_vmem,
        ]
        + [in_vmem] * count,
        out_shape=[
            jax.ShapeDtypeStruct((GROUPS, rows * GHEADS, BIN), bf16),
            jax.ShapeDtypeStruct((D, rows), bf16),
            jax.ShapeDtypeStruct((2 * D, rows), bf16),
        ]
        + [jax.ShapeDtypeStruct(shape, f32) for shape in shapes],
        scratch_shapes=[
            pltpu.VMEM((GWIDTH, BIN), f32),
            pltpu.VMEM((GWIDTH, BIN), f32),
            pltpu.VMEM((GROUPS, 2, GWIDTH, BIN), bf16),
            pltpu.VMEM((GROUPS, 2, 2, GWIDTH, rows), bf16),
            pltpu.VMEM((GROUPS, 2, GWIDTH, rows), bf16),
            pltpu.SemaphoreType.DMA((4 * GROUPS,)),
            pltpu.SemaphoreType.DMA((4 * GROUPS,)),
            pltpu.SemaphoreType.DMA((2 * GROUPS,)),
            pltpu.SemaphoreType.DMA((2 * GROUPS,)),
        ]
        + (scatter_scratch(sizes, plan) if count else []),
        compiler_params=pltpu.CompilerParams(
            collective_id=collective, has_side_effects=True, vmem_limit_bytes=VMEM_LIMIT
        ),
        name="attention_backward",
    )(q_t, go_t, kv_t, kv_t, prob, *tables, *[array.reshape(sizes + shape) for array, shape in zip(arrays, shapes)])


def norm_parts(values):
    middle = values - jnp.mean(values, axis=-1, keepdims=True)
    scale = lax.rsqrt(jnp.mean(middle * middle, axis=-1, keepdims=True) + norm_eps)
    return middle * scale, scale


def norm_back(grad, gain, normal, scale):
    inner = grad * gain
    mean = jnp.mean(inner, axis=-1, keepdims=True)
    along = jnp.mean(inner * normal, axis=-1, keepdims=True)
    return scale * (inner - mean - normal * along)


def column_sums(values):
    return jnp.sum(values, axis=0, keepdims=True)


def feed_kernel(
    steps,
    stream_ref,
    mixed_ref,
    w_out,
    gain,
    shift,
    bias_back,
    cotangent,
    w_in,
    bias_in,
    w_back,
    output_ref,
    grad_in_ref,
    grad_back_ref,
    grad_bias_in_ref,
    grad_stream_ref,
    grad_out_ref,
    grad_mixed_ref,
    grad_gain_ref,
    grad_shift_ref,
    grad_bias_back_ref,
    normal_scr,
    scale_scr,
    second_scr,
    second_t,
    total_scr,
    grad_scr,
):
    step = pl.program_id(0)

    @pl.when(step == 0)
    def _():
        stream = stream_ref[...] + rows_dot(mixed_ref[...], w_out[...])
        normal, scale = norm_parts(stream)
        normal_scr[...] = normal
        scale_scr[...] = jnp.broadcast_to(scale, scale_scr.shape)
        second = (normal * gain[...] + shift[...]).astype(bf16)
        second_scr[...] = second
        second_t[...] = second.T
        total_scr[...] = stream + bias_back[...]
        grad_scr[...] = jnp.zeros_like(grad_scr)

    grad_branch = cotangent[...]
    pre = dot(second_scr[...], w_in[...]) + bias_in[...]
    share = 0.5 * (1.0 + lax.erf(pre * (0.5**0.5)))
    slope = share + pre * (jnp.exp(-0.5 * pre * pre) * (1.0 / math.sqrt(2.0 * math.pi)))
    act = (pre * share).astype(bf16)
    grad_pre = (lanes_dot(grad_branch, w_back[...]) * slope).astype(bf16)
    total_scr[...] += dot(act, w_back[...])
    grad_scr[...] += lanes_dot(grad_pre, w_in[...])
    grad_in_ref[...] = dot(second_t[...], grad_pre).astype(bf16)
    grad_back_ref[...] = rows_dot(act, grad_branch).astype(bf16)
    grad_bias_in_ref[...] = column_sums(grad_pre.astype(f32))

    @pl.when(step == steps - 1)
    def _():
        output_ref[...] = total_scr[...].astype(bf16)
        grad_output = grad_branch.astype(f32)
        grad_second, normal = grad_scr[...], normal_scr[...]
        grad_stream = grad_output + norm_back(grad_second, gain[...], normal, scale_scr[:, 0:1])
        grad_stream_ref[...] = grad_stream
        grad_attn = grad_stream.astype(bf16)
        grad_out_ref[...] = dot(mixed_ref[...], grad_attn).astype(bf16)
        grad_mixed_ref[...] = lanes_dot(w_out[...], grad_attn).astype(bf16)
        grad_gain_ref[...] = column_sums(grad_second * normal)
        grad_shift_ref[...] = column_sums(grad_second)
        grad_bias_back_ref[...] = column_sums(grad_output)


def feed_call(stream_zero, mixed_t, w_out, gain, shift, bias_back, cotangent, w_in, bias_in, w_back):
    rows, hidden = stream_zero.shape[0], w_in.shape[1]
    steps = hidden // FEED_LANES
    row = jax.ShapeDtypeStruct((1, D), f32)
    return pl.pallas_call(
        partial(feed_kernel, steps),
        grid=(steps,),
        in_specs=[in_vmem] * 7
        + [
            pl.BlockSpec((D, FEED_LANES), lambda i: (0, i)),
            pl.BlockSpec((1, FEED_LANES), lambda i: (0, i)),
            pl.BlockSpec((FEED_LANES, D), lambda i: (i, 0)),
        ],
        out_specs=[
            in_vmem,
            pl.BlockSpec((D, FEED_LANES), lambda i: (0, i)),
            pl.BlockSpec((FEED_LANES, D), lambda i: (i, 0)),
            pl.BlockSpec((1, FEED_LANES), lambda i: (0, i)),
        ]
        + [in_vmem] * 6,
        out_shape=[
            jax.ShapeDtypeStruct((rows, D), bf16),
            jax.ShapeDtypeStruct((D, hidden), bf16),
            jax.ShapeDtypeStruct((hidden, D), bf16),
            jax.ShapeDtypeStruct((1, hidden), f32),
            jax.ShapeDtypeStruct((rows, D), f32),
            jax.ShapeDtypeStruct((D, D), bf16),
            jax.ShapeDtypeStruct((D, rows), bf16),
            row,
            row,
            row,
        ],
        scratch_shapes=[
            pltpu.VMEM((rows, D), f32),
            pltpu.VMEM((rows, 128), f32),
            pltpu.VMEM((rows, D), bf16),
            pltpu.VMEM((D, rows), bf16),
            pltpu.VMEM((rows, D), f32),
            pltpu.VMEM((rows, D), f32),
        ],
        compiler_params=pltpu.CompilerParams(vmem_limit_bytes=VMEM_LIMIT),
        name="feed_forward",
    )(stream_zero, mixed_t, w_out, gain, shift, bias_back, cotangent, w_in, bias_in, w_back)


def kernel_gradients(sums, weight_t, mean, width):
    weight_t = weight_t.astype(f32)
    shifted = mean - center
    zeroth, once, twice = (
        jnp.sum(weight_t * sums[at * HEADS : at * HEADS + HEADS], axis=0, keepdims=True) for at in range(3)
    )
    grad_mean = (once - shifted * zeroth) / (width * width)
    grad_width = (twice - 2.0 * shifted * once + shifted * shifted * zeroth) / (width * width * width) - zeroth / width
    return sums[:HEADS], grad_mean, grad_width


def split_small(small, own_hidden):
    rows = small.shape[0]
    vectors = small[:, TFREQ:].T
    return (small[:, :TFREQ].T, *(vectors[at : at + 1] for at in range(5)), vectors[5 : 5 + own_hidden // rows])


def pair_grad_kernel(sizes, plan, count, steps, gs_ref, dist_ref, phi_ref, *refs):
    sources, refs = refs[:count], refs[count:]
    sum_ref, refs = refs[0], refs[1:]
    results, refs = refs[:count], refs[count:]
    (terms, sums), refs = refs[:2], refs[2:]
    step = pl.program_id(0)
    place = my_place(sizes)
    if count:
        total_slots, total_send, total_recv, scratch = refs[:4], refs[4], refs[5], refs[6:]
        total = TotalPart(sums, sum_ref, total_slots, total_send, total_recv, place, sizes)
        opening, turns, closing = stage_turns(scatter_groups(plan, sources, results, scratch, place, sizes))
        tail = min(LAST_TURNS, len(turns))

    @pl.when(step == 0)
    def _():
        sums[...] = jnp.zeros_like(sums)
        if count:
            meet(axis_partners(place, sizes), sizes)
            opening()

    if count:
        spread_turns(step, steps, turns[: len(turns) - tail], 0, 2)

    for u in range(GRAD_ROWS):
        lanes = slice(u * BIN, u * BIN + BIN)
        dist = dist_ref[u : u + 1, :] - center
        for g in range(0, GROUPS, 2):
            low = gs_ref[g, u * GHEADS : u * GHEADS + GHEADS, :].astype(f32)
            high = gs_ref[g + 1, u * GHEADS : u * GHEADS + GHEADS, :].astype(f32)
            grad = jnp.concatenate([low, high], axis=0)
            once = grad * dist
            twice = once * dist
            once_top = once.astype(bf16)
            twice_top = twice.astype(bf16)
            kinds = (
                grad.astype(bf16),
                once_top,
                (once - once_top.astype(f32)).astype(bf16),
                twice_top,
                (twice - twice_top.astype(f32)).astype(bf16),
            )
            for at, kind in enumerate(kinds):
                terms[at * HEADS + g * GHEADS : at * HEADS + (g + 2) * GHEADS, lanes] = kind
    if count:
        spread_turns(step, steps, turns[: len(turns) - tail], 1, 2)

    found = None
    for half in range(GRAD_ROWS // PAIR_ROWS):
        wide = PAIR_ROWS * BIN
        more = lanes_dot(terms[:, half * wide : half * wide + wide], phi_ref[half])
        found = more if found is None else found + more
    sums[:HEADS] += found[:HEADS]
    sums[HEADS : 2 * HEADS] += found[HEADS : 2 * HEADS] + found[2 * HEADS : 3 * HEADS]
    sums[2 * HEADS :] += found[3 * HEADS : 4 * HEADS] + found[4 * HEADS :]

    @pl.when(step == steps - 1)
    def _():
        if not count:
            sum_ref[...] = sums[...]
            return
        total.start(0)
        for at in range(max(tail, 4)):
            if at < tail:
                turns[len(turns) - tail + at]()
            if at < 4:
                total.arrive(at)
                if at < 3:
                    total.start(at + 1)
        closing()
        total.finish()


def pair_grad_call(sizes, gs, dist, phi, arrays, collective):
    rows = dist.shape[0]
    steps = rows // GRAD_ROWS
    count = len(arrays)
    shapes = scatter_shapes(sizes, arrays)
    plan = scatter_plan(shapes)
    total = (3 * HEADS, KERN)
    scratch = [pltpu.VMEM((5 * HEADS, GRAD_ROWS * BIN), bf16), pltpu.VMEM(total, f32)]
    remote = {}
    if count:
        scratch += [pltpu.VMEM((sizes[axis],) + total, f32) for axis in (3, 2, 1, 0)]
        scratch += [pltpu.SemaphoreType.DMA((1, slot_count(sizes)))] * 2
        scratch += scatter_scratch(sizes, plan)
        remote = dict(collective_id=collective, has_side_effects=True)
    return pl.pallas_call(
        partial(pair_grad_kernel, sizes, plan, count, steps),
        grid=(steps,),
        in_specs=[
            pl.BlockSpec((GROUPS, GRAD_ROWS * GHEADS, BIN), lambda i: (0, i, 0)),
            pl.BlockSpec((GRAD_ROWS, BIN), lambda i: (i, 0)),
            pl.BlockSpec((GRAD_ROWS // PAIR_ROWS, KERN, PAIR_ROWS * BIN), lambda i: (i, 0, 0)),
        ]
        + [anywhere] * count,
        out_specs=[in_vmem] * (count + 1),
        out_shape=[jax.ShapeDtypeStruct(total, f32)] + [jax.ShapeDtypeStruct(shape, f32) for shape in shapes],
        scratch_shapes=scratch,
        compiler_params=pltpu.CompilerParams(vmem_limit_bytes=VMEM_LIMIT, **remote),
        name="pair_gradient",
    )(gs, dist, phi, *[array.reshape(sizes + shape) for array, shape in zip(arrays, shapes)])


def settle_kernel(own_hidden, count, sums, weight_t, mean, width, small, *refs):
    values = list(kernel_gradients(sums[...], weight_t[...], mean[...], width[...]))
    values[0] = values[0].T
    values += split_small(small[...], own_hidden)
    for ref, value in zip(refs[count : count + len(values)], values):
        ref[...] = value
    for source, goal in zip(refs[:count], refs[count + len(values) :]):
        goal[...] = source[...]


def settle_call(sums, weight_t, mean, width, small, arrays, own_hidden):
    own = small.shape[0]
    shapes = [(KERN, HEADS), (1, KERN), (1, KERN), (TFREQ, own)] + [(1, own)] * 5 + [(own_hidden // own, own)]
    shapes += [array.shape for array in arrays]
    found = pl.pallas_call(
        partial(settle_kernel, own_hidden, len(arrays)),
        in_specs=[in_vmem] * (5 + len(arrays)),
        out_specs=[in_vmem] * len(shapes),
        out_shape=[jax.ShapeDtypeStruct(shape, f32) for shape in shapes],
        compiler_params=pltpu.CompilerParams(vmem_limit_bytes=VMEM_LIMIT),
        name="settle_gradients",
    )(sums, weight_t, mean, width, small, *arrays)
    return found[:3], found[3:10], found[10:]


def layer_norm(values, norm_gain, norm_offset):
    middle = values - jnp.mean(values, axis=-1, keepdims=True)
    spread = jnp.mean(middle * middle, axis=-1, keepdims=True)
    return middle * lax.rsqrt(spread + norm_eps) * norm_gain + norm_offset


def time_features(time_values):
    half_count = TFREQ // 2
    frequency = jnp.exp(jnp.arange(half_count, dtype=f32) * (-math.log(10000.0) / half_count))
    angles = (1000.0 * time_values)[:, None] * frequency[None, :]
    return jnp.concatenate([jnp.sin(angles), jnp.cos(angles)], axis=1)


def all_scattered(arrays):
    return [lax.psum_scatter(array.astype(f32), ("grp", "dev"), scatter_dimension=0, tiled=True) for array in arrays]


def shards(
    sizes,
    atoms,
    positions,
    segment,
    item_time,
    time_weight,
    norm1_gain,
    norm1_bias,
    qkv_weight,
    out_weight,
    norm2_gain,
    norm2_bias,
    ffn_in,
    ffn_in_bias,
    ffn_out,
    ffn_out_bias,
    pair_weight,
    kernel_mean,
    kernel_width,
    cotangent,
):
    axes = ("grp", "dev")
    own_rows, own_hidden = norm1_gain.shape[0], ffn_in_bias.shape[0]
    mean, width, weight_t = kernel_mean[None], kernel_width[None], pair_weight.T
    vectors = [v[None] for v in (norm1_gain, norm1_bias, norm2_gain, norm2_bias, ffn_out_bias, ffn_in_bias)]
    dist, phi, bias, (small, w_qkv, w_in) = pair_call(
        sizes,
        positions,
        segment.astype(f32)[None],
        mean,
        width,
        weight_t,
        time_weight,
        vectors,
        (qkv_weight, ffn_in,),
        1,
    )
    tables = spread_tables()
    w_qkv, w_in = (full.reshape(-1, full.shape[2]) for full in (w_qkv, w_in))
    w_time_t = small[:, :own_rows].reshape(-1, TFREQ)
    vectors = small[:, own_rows:].astype(f32).transpose(1, 0, 2)
    gain_one, shift_one, gain_two, shift_two, bias_back = (vectors[at, :, :own_rows].reshape(-1) for at in range(5))
    bias_in = vectors[5, :, :own_hidden].reshape(-1)

    features = time_features(item_time).astype(bf16)
    stream_zero = atoms.astype(f32) + lanes_dot(features, w_time_t)
    normed = layer_norm(stream_zero, gain_one, shift_one).astype(bf16)
    packed_t = lax.dot_general(w_qkv, normed, (((0,), (1,)), ((), ())), preferred_element_type=f32).astype(bf16)
    q_t = packed_t[:D]
    mixed_t, prob, kv_t, (w_out, w_back) = forward_call(
        sizes, q_t, packed_t[D:], bias, tables, (out_weight, ffn_out), 5
    )

    (
        output,
        grad_in,
        grad_back,
        grad_bias_in,
        grad_stream_one,
        grad_out_weight,
        grad_mixed_t,
        grad_gain_two,
        grad_shift_two,
        grad_bias_back,
    ) = feed_call(
        stream_zero, mixed_t, w_out, gain_two[None], shift_two[None], bias_back[None], cotangent, w_in, bias_in[None], w_back
    )
    grad_gain_two, grad_shift_two, grad_bias_back = grad_gain_two[0], grad_shift_two[0], grad_bias_back[0]

    own_sums = own_rows % 8 == 0
    early = (grad_back,) if own_sums else ()
    gs, grad_query_t, own, *early_sums = backward_call(sizes, q_t, grad_mixed_t, kv_t, prob, tables, early, 2)
    grad_packed_t = jnp.concatenate([grad_query_t, own], axis=0)
    grad_qkv = lax.dot_general(normed, grad_packed_t, (((0,), (1,)), ((), ())), preferred_element_type=f32).astype(bf16)
    grad_normed = lax.dot_general(grad_packed_t, w_qkv, (((0,), (1,)), ((), ())), preferred_element_type=f32)
    _, norm_one_pull = jax.vjp(layer_norm, stream_zero, gain_one, shift_one)
    grad_zero_part, grad_gain_one, grad_shift_one = norm_one_pull(grad_normed)
    grad_input = grad_stream_one + grad_zero_part
    grad_time_t = rows_dot(grad_input.astype(bf16), features).astype(bf16)

    vectors = jnp.stack([grad_gain_one, grad_shift_one, grad_gain_two, grad_shift_two, grad_bias_back], axis=1)
    vectors = jnp.concatenate([vectors, grad_bias_in.reshape(D // own_rows, -1, own_rows).transpose(0, 2, 1).reshape(D, -1)], axis=1)
    vectors = jnp.pad(vectors, ((0, 0), (0, 128 - vectors.shape[1]))).astype(bf16)
    grad_small = jnp.concatenate([grad_time_t, vectors], axis=1)
    late = (grad_in, grad_out_weight, grad_qkv, grad_small) if own_sums else ()
    sums, *late_sums = pair_grad_call(sizes, gs, dist, phi, late, 3)
    if own_sums:
        grad_small, weight_sums = late_sums[3], (*early_sums, *late_sums[:3])
    else:
        *weight_sums, grad_small = all_scattered((grad_back, grad_in, grad_out_weight, grad_qkv, grad_small))
        sums = lax.psum(sums, axes)
    (grad_pair, grad_mean, grad_width), small_grads, weight_sums = settle_call(
        sums, weight_t, mean, width, grad_small, weight_sums, own_hidden
    )
    grad_back, grad_in, grad_out_weight, grad_qkv = weight_sums
    grad_time, *vector_grads, grad_hidden = small_grads
    grad_gain_one, grad_shift_one, grad_gain_two, grad_shift_two, grad_bias_back = (row[0] for row in vector_grads)
    return (
        output,
        grad_input,
        grad_time,
        grad_gain_one,
        grad_shift_one,
        grad_qkv,
        grad_out_weight,
        grad_gain_two,
        grad_shift_two,
        grad_in,
        grad_hidden.reshape(-1),
        grad_back,
        grad_bias_back,
        grad_pair,
        grad_mean[0],
        grad_width[0],
    )


def solution(mesh):
    in_specs = (
        P(("grp", "dev"), None),
        P(None, ("grp", "dev")),
        P(("grp", "dev")),
        P(("grp", "dev")),
        P(None, ("grp", "dev")),
        P(("grp", "dev")),
        P(("grp", "dev")),
        P(("grp", "dev"), None),
        P(("grp", "dev"), None),
        P(("grp", "dev")),
        P(("grp", "dev")),
        P(("grp", "dev"), None),
        P(("grp", "dev")),
        P(("grp", "dev"), None),
        P(("grp", "dev")),
        P(),
        P(),
        P(),
        P(("grp", "dev"), None),
    )
    out_specs = (
        P(("grp", "dev"), None),
        P(("grp", "dev"), None),
        P(None, ("grp", "dev")),
        P(("grp", "dev")),
        P(("grp", "dev")),
        P(("grp", "dev"), None),
        P(("grp", "dev"), None),
        P(("grp", "dev")),
        P(("grp", "dev")),
        P(("grp", "dev"), None),
        P(("grp", "dev")),
        P(("grp", "dev"), None),
        P(("grp", "dev")),
        P(),
        P(),
        P(),
    )
    return jax.shard_map(partial(shards, grid_of_mesh(mesh)), mesh=mesh, in_specs=in_specs, out_specs=out_specs, check_vma=False)
```

profile of v0, /device:TPU:0, one launch (start us, length us, event | category | flops | bytes accessed | tf_op | source)
XLA Modules:
  0.0 304.8 jit_solution(4947463725549503231)
XLA Ops:
  0.7 1.2 convert_element_type.27
  1.9 0.7 broadcast_multiply_fusion.1
  2.6 1.4 copy.51.time_weight
  4.0 0.3 fusion.3
  4.3 74.8 %pair_bias_and_gather.1 = (f32[256,1024]{1,0:T(8,128)}, bf16[16,128,16384]{2,1,0:T(8,128)(2,1)}, f32[4,2048,1024]{2,1,0:T(8,128)}, bf16[4,2,2,2,32,128]{5,4,3,2,...) custom-call(f32[3,256]{1,0:T(4,128)} %positions.1, ...), custom_call_target="tpu_custom_call" | custom-call | tf_op jit(solution)/shard_map/pair_bias_and_gather/pallas_call | solution.py:487
  79.1 0.8 slice.41
  80.0 0.9 slice.40
  81.0 0.7 broadcast_in_dim_reshape_squeeze.18.bias_in
  81.7 0.7 broadcast_in_dim_reshape_squeeze.17.bias_back
  82.3 0.7 broadcast_in_dim_reshape_squeeze.16.shift
  83.0 0.7 broadcast_in_dim_reshape_squeeze.15.gain
  83.7 0.1 mul.102
  83.8 0.1 add.31
  83.8 1.4 fusion.10
  85.2 0.2 multiply_reduce_fusion.2
  85.5 3.3 %convolution_convert_fusion.1 = bf16[2304,256]{1,0:T(8,128)(2,1)S(1)} fusion(bf16[768,2304]{1,0:T(8,128)(2,1)} %bitcast.69, f32[256,768]{1,0:T(8,128)S(1)} %get-tuple-element.165.stream_ref, f32[768]{0:T(1024)S(1)} %add.31, f32[768]{0:T(1024)S(1)} %mul.102, f32[256]{0:T(256)S(1)} %fusion.5, f32[256]{0:T(256)S(1)} %broadcast_multiply_fusion), kind=kOutput, calls=%fused_computation.1 | convolution fusion | flops 907542528 | bytes 5513216 | tf_op jit(solution)/shard_map/dot_general | solution.py:1246
  88.8 0.0 copy-done
  88.8 0.8 slice.44.q_ref
  89.5 0.9 slice.45.own_ref
  90.5 55.7 %attention_forward.1 = (bf16[768,256]{1,0:T(8,128)(2,1)}, bf16[4,2048,1024]{2,1,0:T(8,128)(2,1)}, bf16[1536,1024]{1,0:T(8,128)(2,1)}, bf16[4,2,2,2,24,768]{5,4,3...) custom-call(bf16[768,256]{1,0:T(8,128)(2,1)} %slice.44.q_ref, bf16[1536,256]{1,0:T(8,128)(2,1)} %slice.45.own_ref, ...), custom_call_target="tpu_custom_call" | custom-call | tf_op jit(solution)/shard_map/attention_forward/pallas_call | solution.py:682
  146.2 16.5 %feed_forward.1 = (bf16[256,768]{1,0:T(8,128)(2,1)}, bf16[768,3072]{1,0:T(8,128)(2,1)}, bf16[3072,768]{1,0:T(8,128)(2,1)}, f32[1,3072]{1,0:T(1,128)}, f32[256,76...) custom-call(f32[256,768]{1,0:T(8,128)} %copy-done, ...), custom_call_target="tpu_custom_call" | custom-call | tf_op jit(solution)/shard_map/feed_forward/pallas_call | solution.py:995
  162.7 0.0 copy-start.5
  162.7 0.0 copy-start.4
  162.7 0.0 copy-start.6
  162.7 0.0 copy-start.7
  162.7 0.0 copy-start.1
  162.7 57.3 %attention_backward.1 = (bf16[4,2048,1024]{2,1,0:T(8,128)(2,1)}, bf16[768,256]{1,0:T(8,128)(2,1)}, bf16[1536,256]{1,0:T(8,128)(2,1)}, f32[96,768]{1,0:T(8,128)}) custom-call(bf16[768,256]{1,0:T(8,128)(2,1)} %slice.44.q_ref, bf16[768,256]{1,0:T(8,128)(2,1)} %get-tuple-element.69.go_ref, bf16[1536,1024]{1,0:T(8,128)(2,1)} %get-tuple-element.70.k_ref.v_ref, ...), custom_call_target="tpu_custom_call" | custom-call | tf_op jit(solution)/shard_map/attention_backward/pallas_call | solution.py:861
  220.0 0.0 copy-done.5
  220.1 0.0 copy-done.4
  220.1 0.0 copy-done.6
  220.1 0.0 copy-done.7
  220.2 0.1 reshape.118
  220.3 0.1 reshape.119
  220.4 1.0 constant_dynamic-update-slice_fusion.1
  221.4 1.2 constant_dynamic-update-slice_fusion
  222.6 3.4 %multiply_reduce_fusion = (bf16[768]{0:T(1024)(128)(2,1)S(1)}, f32[256]{0:T(256)S(1)}, bf16[768]{0:T(1024)(128)(2,1)S(1)}, f32[256,768]{1,0:T(8,128)S(1)}) fusion(f32[256,768]{1,0:T(8,128)S(1)} %copy-done.1, f32[256]{0:T(256)S(1)} %fusion.5, f32[256]{0:T(256)S(1)} %broadcast_multiply_fusion, f32[768]{0:T(1024)S(1)} %mul.102, ...), kind=kOutput, calls=%fused_computation.6 | convolution fusion | flops 907540736 | bytes 6300672 | tf_op jit(solution)/shard_map/dot_general | solution.py:1273
  226.0 0.3 fusion.8
  226.4 0.2 add_add_fusion.1
  226.6 0.0 copy-start.2
  226.6 0.4 concatenate.16
  227.0 0.2 convolution_convert_fusion.2
  227.2 1.0 copy.54
  228.2 3.0 convolution_convert_fusion
  231.2 66.9 %pair_gradient.1 = (f32[96,128]{1,0:T(8,128)}, f32[24,3072]{1,0:T(8,128)}, f32[24,768]{1,0:T(8,128)}, f32[24,2304]{1,0:T(8,128)}, f32[24,256]{1,0:T(8,128)}) custom-call(bf16[4,2048,1024]{2,1,0:T(8,128)(2,1)} %get-tuple-element.75.gs_ref, f32[256,1024]{1,0:T(8,128)} %get-tuple-element.76.dist_ref, bf16[16,128,16384]{2,1,0:T(8,128)(2,1)} %get-tuple-element.77.phi_ref, ...), custom_call_target="tpu_custom_call" | custom-call | tf_op jit(solution)/shard_map/pair_gradient/pallas_call | solution.py:1139
  298.2 2.3 settle_gradients.1
  300.5 1.5 copy.55
  302.0 1.3 reshape.121
  303.3 1.5 copy.56
  (20 shorter events, 0.2 us)
Async XLA Ops:
  85.2 3.5 %copy-start = (f32[256,768]{1,0:T(8,128)}, f32[256,768]{1,0:T(8,128)S(1)}, u32[]{:S(2)}) copy-start(f32[256,768]{1,0:T(8,128)S(1)} %get-tuple-element.165.stream_ref) | copy-start | bytes 2359300
  162.7 57.4 %copy-start.5 = (f32[1,768]{1,0:T(1,128)S(1)}, f32[1,768]{1,0:T(1,128)}, u32[]{:S(2)}) copy-start(f32[1,768]{1,0:T(1,128)} %get-tuple-element.80) | copy-start | bytes 9220
  162.7 57.4 %copy-start.4 = (f32[1,3072]{1,0:T(1,128)S(1)}, f32[1,3072]{1,0:T(1,128)}, u32[]{:S(2)}) copy-start(f32[1,3072]{1,0:T(1,128)} %get-tuple-element.83) | copy-start | bytes 36868
  162.7 57.4 %copy-start.6 = (f32[1,768]{1,0:T(1,128)S(1)}, f32[1,768]{1,0:T(1,128)}, u32[]{:S(2)}) copy-start(f32[1,768]{1,0:T(1,128)} %get-tuple-element.81) | copy-start | bytes 9220
  162.7 57.4 %copy-start.7 = (f32[1,768]{1,0:T(1,128)S(1)}, f32[1,768]{1,0:T(1,128)}, u32[]{:S(2)}) copy-start(f32[1,768]{1,0:T(1,128)} %get-tuple-element.82) | copy-start | bytes 9220
  162.7 59.9 %copy-start.1 = (f32[256,768]{1,0:T(8,128)S(1)}, f32[256,768]{1,0:T(8,128)}, u32[]{:S(2)}) copy-start(f32[256,768]{1,0:T(8,128)} %copy-done) | copy-start | bytes 2359300
  222.6 3.8 %copy-start.3 = (f32[256,768]{1,0:T(8,128)S(1)}, f32[256,768]{1,0:T(8,128)}, u32[]{:S(2)}) copy-start(f32[256,768]{1,0:T(8,128)} %get-tuple-element.68) | copy-start | bytes 2359300
  226.6 4.7 %copy-start.2 = (f32[256,768]{1,0:T(8,128)}, f32[256,768]{1,0:T(8,128)S(1)}, u32[]{:S(2)}) copy-start(f32[256,768]{1,0:T(8,128)S(1)} %add_add_fusion.1) | copy-start | bytes 2359300
where the time goes:
time: 306 us; the launch traced here: 305 us
  Pallas kernels  274 us (90%)
  local copies, waits for them, and re-layouts  15.9 us (5%)
  matrix products  11.3 us (4%)
  other arithmetic  3.07 us (1%)
    pallas_call x1, Pallas kernels, pair_call(): pl.pallas_call(partial(pair_kernel, sizes, plan, count, steps), grid=(ste...  74.8 us
    pallas_call x1, Pallas kernels, pair_grad_call(): pl.pallas_call(partial(pair_grad_kernel, sizes, plan, count, steps), grid...  66.9 us
    pallas_call x1, Pallas kernels, backward_call(): pl.pallas_call(partial(backward_kernel, sizes, plan, count, GROUPS * part...  57.3 us
    pallas_call x1, Pallas kernels, forward_call(): pl.pallas_call(partial(forward_kernel, sizes, plan, count, parts), grid=(...  55.7 us
    pallas_call x1, Pallas kernels, feed_call(): pl.pallas_call(partial(feed_kernel, steps), grid=(steps,), in_specs=[in_v...  16.5 us

commit v1 on v0

--- a/solution.py
+++ b/solution.py
@@ -445,8 +445,8 @@
         mask_scr[...] = jnp.zeros_like(mask_scr)
         for at, vector in enumerate(vectors):
             mask_scr[at : at + 1, pl.ds(0, vector.shape[1])] = vector[...].astype(f32)
-        rest = mask_scr[0 : sources[0].shape[0] - time_weight.shape[1], pl.ds(0, TFREQ)]
-        sources[0][...] = jnp.concatenate([time_weight[...].astype(f32).T, rest], axis=0).astype(bf16)
+        rest = mask_scr[0 : sources[0].shape[0] - time_weight.shape[0], pl.ds(0, TFREQ)]
+        sources[0][...] = jnp.concatenate([time_weight[...].astype(f32), rest], axis=0).astype(bf16)
         meet(axis_partners(place, sizes) + [block_partners(place)[2]], sizes)
         for copy in own:
             copy.start()
@@ -480,7 +480,7 @@
     rows = positions.shape[1]
     count = 1 + len(arrays)
     steps = rows // PAIR_ROWS
-    own = time_weight.shape[1]
+    own = time_weight.shape[0]
     small = jax.ShapeDtypeStruct((own + 8, TFREQ), bf16)
     plan = gather_plan([array.shape for array in (small, *arrays)])
     parts, slots = part_count(plan), slot_count(sizes)
@@ -540,13 +540,16 @@
     def rows(self, g, which):
         return pl.ds(which * D + g * GWIDTH, GWIDTH)
 
+    def own_rows(self, g, which):
+        return pl.ds((1 + which) * D + g * GWIDTH, GWIDTH)
+
     def lanes(self, at):
         return pl.ds(at * self.width, self.width)
 
     def far(self, g):
         return [
             send(
-                self.own.at[self.rows(g, which)],
+                self.own.at[self.own_rows(g, which)],
                 self.full.at[self.rows(g, which), self.lanes(2)],
                 self.far_sems,
                 g * 2 + which,
@@ -559,7 +562,7 @@
     def near(self, g):
         return [
             send(
-                self.own.at[self.rows(g, which)],
+                self.own.at[self.own_rows(g, which)],
                 self.full.at[self.rows(g, which), self.lanes(1)],
                 self.near_sems,
                 g * 2 + which,
@@ -628,7 +631,7 @@
         @pl.when((group == g) & (part == 0))
         def _():
             if g == 0:
-                kv_ref[:, pl.ds(0, share.width)] = own_ref[...]
+                kv_ref[:, pl.ds(0, share.width)] = own_ref[pl.ds(D, 2 * D), :]
                 meet(axis_partners(place, sizes), sizes)
                 share.open()
                 for copy in held:
@@ -672,8 +675,8 @@
             copy.wait()
 
 
-def forward_call(sizes, q_t, kv_t, bias, tables, arrays, collective):
-    rows = q_t.shape[1]
+def forward_call(sizes, packed_t, bias, tables, arrays, collective):
+    rows = packed_t.shape[1]
     wide = ATT_ROWS * GHEADS
     parts = rows // ATT_ROWS
     count = len(arrays)
@@ -709,7 +712,7 @@
             collective_id=collective, has_side_effects=True, vmem_limit_bytes=VMEM_LIMIT
         ),
         name="attention_forward",
-    )(q_t, kv_t, bias, *tables, *arrays)
+    )(packed_t, packed_t, bias, *tables, *arrays)
     return outs[0], outs[1], outs[2], [full.reshape((-1, full.shape[-1])) for full in outs[3:]]
 
 
@@ -763,7 +766,7 @@
         for which in range(2):
             total = self.block(g, which, 0)[...].astype(f32) + self.near[g, which, 0].astype(f32)
             total = total + self.far[g, which].astype(f32)
-            self.result[pl.ds(which * D + g * GWIDTH, GWIDTH), :] = total.astype(bf16)
+            self.result[pl.ds((1 + which) * D + g * GWIDTH, GWIDTH), :] = total.astype(bf16)
 
     def finish(self):
         for g in range(GROUPS):
@@ -775,7 +778,7 @@
     sizes, plan, count, steps, q_ref, go_ref, k_ref, v_ref, prob_ref, spread, gather, head, head_t, *refs
 ):
     sources, refs = refs[:count], refs[count:]
-    (gs_ref, gq_ref, own_ref), refs = refs[:3], refs[3:]
+    (gs_ref, own_ref), refs = refs[:2], refs[2:]
     results, refs = refs[:count], refs[count:]
     (key_sum, value_sum, outbox, near, far), refs = refs[:5], refs[5:]
     near_sems, far_sems, scratch = refs[:2], refs[2:4], refs[4:]
@@ -817,7 +820,10 @@
         spread_turns(step, steps, turns, 1, 2)
 
     grad_query = lanes_dot(k_ref[...], gs_ref[0]) * (HDIM**-0.5)
-    gq_ref[...] = lanes_dot(grad_query.astype(bf16) * head_t[...], gather[...]).astype(bf16)
+    rows, lanes = pl.multiple_of(group * GWIDTH, GWIDTH), pl.multiple_of(part * ATT_ROWS, ATT_ROWS)
+    own_ref[pl.ds(rows, GWIDTH), pl.ds(lanes, ATT_ROWS)] = lanes_dot(
+        grad_query.astype(bf16) * head_t[...], gather[...]
+    ).astype(bf16)
     query_t = lanes_dot(q_ref[...], spread[...]).astype(bf16) * head_t[...]
     grad_out_t = lanes_dot(go_ref[...], spread[...]).astype(bf16) * head_t[...]
     grad_key = dot(query_t, gs_ref[0])
@@ -872,14 +878,12 @@
         + [anywhere] * count,
         out_specs=[
             pl.BlockSpec((1, wide, BIN), lambda g, i: (g, i, 0)),
-            pl.BlockSpec((GWIDTH, ATT_ROWS), lambda g, i: (g, i)),
             in_vmem,
         ]
         + [in_vmem] * count,
         out_shape=[
             jax.ShapeDtypeStruct((GROUPS, rows * GHEADS, BIN), bf16),
-            jax.ShapeDtypeStruct((D, rows), bf16),
-            jax.ShapeDtypeStruct((2 * D, rows), bf16),
+            jax.ShapeDtypeStruct((3 * D, rows), bf16),
         ]
         + [jax.ShapeDtypeStruct(shape, f32) for shape in shapes],
         scratch_shapes=[
@@ -923,9 +927,7 @@
     stream_ref,
     mixed_ref,
     w_out,
-    gain,
-    shift,
-    bias_back,
+    vectors,
     cotangent,
     w_in,
     bias_in,
@@ -948,6 +950,7 @@
     grad_scr,
 ):
     step = pl.program_id(0)
+    gain, shift, bias_back = (vectors.at[pl.ds(at, 1)] for at in range(3))
 
     @pl.when(step == 0)
     def _():
@@ -988,14 +991,14 @@
         grad_bias_back_ref[...] = column_sums(grad_output)
 
 
-def feed_call(stream_zero, mixed_t, w_out, gain, shift, bias_back, cotangent, w_in, bias_in, w_back):
+def feed_call(stream_zero, mixed_t, w_out, vectors, cotangent, w_in, bias_in, w_back):
     rows, hidden = stream_zero.shape[0], w_in.shape[1]
     steps = hidden // FEED_LANES
     row = jax.ShapeDtypeStruct((1, D), f32)
     return pl.pallas_call(
         partial(feed_kernel, steps),
         grid=(steps,),
-        in_specs=[in_vmem] * 7
+        in_specs=[in_vmem] * 5
         + [
             pl.BlockSpec((D, FEED_LANES), lambda i: (0, i)),
             pl.BlockSpec((1, FEED_LANES), lambda i: (0, i)),
@@ -1030,7 +1033,7 @@
         ],
         compiler_params=pltpu.CompilerParams(vmem_limit_bytes=VMEM_LIMIT),
         name="feed_forward",
-    )(stream_zero, mixed_t, w_out, gain, shift, bias_back, cotangent, w_in, bias_in, w_back)
+    )(stream_zero, mixed_t, w_out, vectors, cotangent, w_in, bias_in, w_back)
 
 
 def kernel_gradients(sums, weight_t, mean, width):
@@ -1047,7 +1050,7 @@
 def split_small(small, own_hidden):
     rows = small.shape[0]
     vectors = small[:, TFREQ:].T
-    return (small[:, :TFREQ].T, *(vectors[at : at + 1] for at in range(5)), vectors[5 : 5 + own_hidden // rows])
+    return (small[:, :TFREQ], *(vectors[at : at + 1] for at in range(5)), vectors[5 : 5 + own_hidden // rows])
 
 
 def pair_grad_kernel(sizes, plan, count, steps, gs_ref, dist_ref, phi_ref, *refs):
@@ -1155,7 +1158,6 @@
 
 def settle_kernel(own_hidden, count, sums, weight_t, mean, width, small, *refs):
     values = list(kernel_gradients(sums[...], weight_t[...], mean[...], width[...]))
-    values[0] = values[0].T
     values += split_small(small[...], own_hidden)
     for ref, value in zip(refs[count : count + len(values)], values):
         ref[...] = value
@@ -1165,7 +1167,7 @@
 
 def settle_call(sums, weight_t, mean, width, small, arrays, own_hidden):
     own = small.shape[0]
-    shapes = [(KERN, HEADS), (1, KERN), (1, KERN), (TFREQ, own)] + [(1, own)] * 5 + [(own_hidden // own, own)]
+    shapes = [(HEADS, KERN), (1, KERN), (1, KERN), (own, TFREQ)] + [(1, own)] * 5 + [(own_hidden // own, own)]
     shapes += [array.shape for array in arrays]
     found = pl.pallas_call(
         partial(settle_kernel, own_hidden, len(arrays)),
@@ -1228,7 +1230,7 @@
         mean,
         width,
         weight_t,
-        time_weight,
+        time_weight.T,
         vectors,
         (qkv_weight, ffn_in,),
         1,
@@ -1237,16 +1239,16 @@
     w_qkv, w_in = (full.reshape(-1, full.shape[2]) for full in (w_qkv, w_in))
     w_time_t = small[:, :own_rows].reshape(-1, TFREQ)
     vectors = small[:, own_rows:].astype(f32).transpose(1, 0, 2)
-    gain_one, shift_one, gain_two, shift_two, bias_back = (vectors[at, :, :own_rows].reshape(-1) for at in range(5))
+    gain_one, shift_one = (vectors[at, :, :own_rows].reshape(-1) for at in range(2))
+    vectors_two = vectors[2:5, :, :own_rows].reshape(3, -1)
     bias_in = vectors[5, :, :own_hidden].reshape(-1)
 
     features = time_features(item_time).astype(bf16)
     stream_zero = atoms.astype(f32) + lanes_dot(features, w_time_t)
     normed = layer_norm(stream_zero, gain_one, shift_one).astype(bf16)
     packed_t = lax.dot_general(w_qkv, normed, (((0,), (1,)), ((), ())), preferred_element_type=f32).astype(bf16)
-    q_t = packed_t[:D]
     mixed_t, prob, kv_t, (w_out, w_back) = forward_call(
-        sizes, q_t, packed_t[D:], bias, tables, (out_weight, ffn_out), 5
+        sizes, packed_t, bias, tables, (out_weight, ffn_out), 5
     )
 
     (
@@ -1261,25 +1263,24 @@
         grad_shift_two,
         grad_bias_back,
     ) = feed_call(
-        stream_zero, mixed_t, w_out, gain_two[None], shift_two[None], bias_back[None], cotangent, w_in, bias_in[None], w_back
+        stream_zero, mixed_t, w_out, vectors_two, cotangent, w_in, bias_in[None], w_back
     )
     grad_gain_two, grad_shift_two, grad_bias_back = grad_gain_two[0], grad_shift_two[0], grad_bias_back[0]
 
     own_sums = own_rows % 8 == 0
     early = (grad_back,) if own_sums else ()
-    gs, grad_query_t, own, *early_sums = backward_call(sizes, q_t, grad_mixed_t, kv_t, prob, tables, early, 2)
-    grad_packed_t = jnp.concatenate([grad_query_t, own], axis=0)
+    gs, grad_packed_t, *early_sums = backward_call(sizes, packed_t, grad_mixed_t, kv_t, prob, tables, early, 2)
     grad_qkv = lax.dot_general(normed, grad_packed_t, (((0,), (1,)), ((), ())), preferred_element_type=f32).astype(bf16)
     grad_normed = lax.dot_general(grad_packed_t, w_qkv, (((0,), (1,)), ((), ())), preferred_element_type=f32)
     _, norm_one_pull = jax.vjp(layer_norm, stream_zero, gain_one, shift_one)
     grad_zero_part, grad_gain_one, grad_shift_one = norm_one_pull(grad_normed)
     grad_input = grad_stream_one + grad_zero_part
-    grad_time_t = rows_dot(grad_input.astype(bf16), features).astype(bf16)
+    grad_time_rows = rows_dot(grad_input.astype(bf16), features).astype(bf16)
 
     vectors = jnp.stack([grad_gain_one, grad_shift_one, grad_gain_two, grad_shift_two, grad_bias_back], axis=1)
     vectors = jnp.concatenate([vectors, grad_bias_in.reshape(D // own_rows, -1, own_rows).transpose(0, 2, 1).reshape(D, -1)], axis=1)
     vectors = jnp.pad(vectors, ((0, 0), (0, 128 - vectors.shape[1]))).astype(bf16)
-    grad_small = jnp.concatenate([grad_time_t, vectors], axis=1)
+    grad_small = jnp.concatenate([grad_time_rows, vectors], axis=1)
     late = (grad_in, grad_out_weight, grad_qkv, grad_small) if own_sums else ()
     sums, *late_sums = pair_grad_call(sizes, gs, dist, phi, late, 3)
     if own_sums:
@@ -1287,16 +1288,16 @@
     else:
         *weight_sums, grad_small = all_scattered((grad_back, grad_in, grad_out_weight, grad_qkv, grad_small))
         sums = lax.psum(sums, axes)
-    (grad_pair, grad_mean, grad_width), small_grads, weight_sums = settle_call(
+    (grad_pair_t, grad_mean, grad_width), small_grads, weight_sums = settle_call(
         sums, weight_t, mean, width, grad_small, weight_sums, own_hidden
     )
     grad_back, grad_in, grad_out_weight, grad_qkv = weight_sums
-    grad_time, *vector_grads, grad_hidden = small_grads
+    grad_time_t, *vector_grads, grad_hidden = small_grads
     grad_gain_one, grad_shift_one, grad_gain_two, grad_shift_two, grad_bias_back = (row[0] for row in vector_grads)
     return (
         output,
         grad_input,
-        grad_time,
+        grad_time_t.T,
         grad_gain_one,
         grad_shift_one,
         grad_qkv,
@@ -1307,7 +1308,7 @@
         grad_hidden.reshape(-1),
         grad_back,
         grad_bias_back,
-        grad_pair,
+        grad_pair_t.T,
         grad_mean[0],
         grad_width[0],
     )

time: 306 us -> 296 us (0.967)
  local copies, waits for them, and re-layouts: 15.9 us -> 6.29 us
    unnamed x20 -> x18, local copies, waits for them, and re-layouts: 5.5 us -> 0.13 us
where the time goes in v1:
time: 296 us
  Pallas kernels  273 us (92%)
  matrix products  12.7 us (4%)
  local copies, waits for them, and re-layouts  6.29 us (2%)
  other arithmetic  3.07 us (1%)
    pallas_call x1, Pallas kernels, pair_call(): pl.pallas_call(partial(pair_kernel, sizes, plan, count, steps), grid=(ste...  74.8 us
    pallas_call x1, Pallas kernels, pair_grad_call(): pl.pallas_call(partial(pair_grad_kernel, sizes, plan, count, steps), grid...  66.9 us
    pallas_call x1, Pallas kernels, backward_call(): pl.pallas_call(partial(backward_kernel, sizes, plan, count, GROUPS * part...  56.8 us
    pallas_call x1, Pallas kernels, forward_call(): pl.pallas_call(partial(forward_kernel, sizes, plan, count, parts), grid=(...  55.5 us
    pallas_call x1, Pallas kernels, feed_call(): pl.pallas_call(partial(feed_kernel, steps), grid=(steps,), in_specs=[in_v...  16.4 us

profile of v1, /device:TPU:0, one launch (start us, length us, event | category | flops | bytes accessed | tf_op | source)
XLA Modules:
  0.0 295.6 jit_solution(8062051454148128165)
XLA Ops:
  0.7 1.2 convert_element_type.27
  1.9 0.7 broadcast_multiply_fusion.1
  2.6 0.3 fusion.3
  2.9 74.8 %pair_bias_and_gather.1 = (f32[256,1024]{1,0:T(8,128)}, bf16[16,128,16384]{2,1,0:T(8,128)(2,1)}, f32[4,2048,1024]{2,1,0:T(8,128)}, bf16[4,2,2,2,32,128]{5,4,3,2,...) custom-call(f32[3,256]{1,0:T(4,128)} %positions.1, ...), custom_call_target="tpu_custom_call" | custom-call | tf_op jit(solution)/shard_map/pair_bias_and_gather/pallas_call | solution.py:487
  77.8 0.8 slice.25
  78.6 0.9 slice.24
  79.6 0.7 broadcast_in_dim_reshape_squeeze.2.bias_in
  80.3 0.7 reshape.116.vectors
  81.0 0.1 mul.102
  81.1 0.1 add.31
  81.1 1.4 fusion.10
  82.5 0.0 copy-start
  82.5 0.2 multiply_reduce_fusion.2
  82.8 4.3 %convolution_convert_fusion.1.q_ref.own_ref = bf16[2304,256]{1,0:T(8,128)(2,1)} fusion(bf16[768,2304]{1,0:T(8,128)(2,1)} %bitcast.73, f32[256,768]{1,0:T(8,128)S(1)} %get-tuple-element.112.stream_ref, f32[768]{0:T(1024)S(1)} %add.31, f32[768]{0:T(1024)S(1)} %mul.102, f32[256]{0:T(256)S(1)} %fusion.5, f32[256]{0:T(256)S(1)} %broadcast_multiply_fusion), kind=kOutput, calls=%fused_computation.1 | convolution fusion | flops 907542528 | bytes 5513216 | tf_op jit(solution)/shard_map/dot_general | solution.py:1249
  87.0 0.0 copy-done
  87.0 55.5 %attention_forward.1 = (bf16[768,256]{1,0:T(8,128)(2,1)}, bf16[4,2048,1024]{2,1,0:T(8,128)(2,1)}, bf16[1536,1024]{1,0:T(8,128)(2,1)}, bf16[4,2,2,2,24,768]{5,4,3...) custom-call(bf16[2304,256]{1,0:T(8,128)(2,1)} %convolution_convert_fusion.1.q_ref.own_ref, ...), custom_call_target="tpu_custom_call" | custom-call | tf_op jit(solution)/shard_map/attention_forward/pallas_call | solution.py:685
  142.5 16.4 %feed_forward.1 = (bf16[256,768]{1,0:T(8,128)(2,1)}, bf16[768,3072]{1,0:T(8,128)(2,1)}, bf16[3072,768]{1,0:T(8,128)(2,1)}, f32[1,3072]{1,0:T(1,128)}, f32[256,76...) custom-call(f32[256,768]{1,0:T(8,128)} %copy-done, ...), custom_call_target="tpu_custom_call" | custom-call | tf_op jit(solution)/shard_map/feed_forward/pallas_call | solution.py:998
  159.0 0.0 copy-start.1
  159.0 56.8 %attention_backward.1 = (bf16[4,2048,1024]{2,1,0:T(8,128)(2,1)}, bf16[2304,256]{1,0:T(8,128)(2,1)}, f32[96,768]{1,0:T(8,128)}) custom-call(bf16[2304,256]{1,0:T(8,128)(2,1)} %convolution_convert_fusion.1.q_ref.own_ref, bf16[768,256]{1,0:T(8,128)(2,1)} %get-tuple-element.68.go_ref, bf16[1536,1024]{1,0:T(8,128)(2,1)} %get-tuple-element.69.k_ref.v_ref, ...), custom_call_target="tpu_custom_call" | custom-call | tf_op jit(solution)/shard_map/attention_backward/pallas_call | solution.py:867
  215.8 0.0 copy-done.1
  215.8 0.0 copy-start.4
  215.8 3.8 %multiply_reduce_fusion = (bf16[768]{0:T(1024)(128)(2,1)S(1)}, f32[256]{0:T(256)S(1)}, bf16[768]{0:T(1024)(128)(2,1)S(1)}, f32[256,768]{1,0:T(8,128)S(1)}) fusion(f32[256,768]{1,0:T(8,128)S(1)} %copy-done.1, f32[256]{0:T(256)S(1)} %fusion.5, f32[256]{0:T(256)S(1)} %broadcast_multiply_fusion, f32[768]{0:T(1024)S(1)} %mul.102, ...), kind=kOutput, calls=%fused_computation.6 | convolution fusion | flops 907540736 | bytes 6300672 | tf_op jit(solution)/shard_map/dot_general | solution.py:1274
  219.6 0.0 copy-start.6
  219.6 0.0 copy-start.5
  219.6 0.0 copy-start.7
  219.6 0.0 copy-start.8
  219.7 0.0 copy-start.3
  219.7 0.3 fusion.8
  220.0 0.0 copy-done.4
  220.0 0.2 add_add_fusion.1
  220.2 0.0 copy-start.2
  220.2 0.1 copy-done.6
  220.3 0.0 copy-done.5
  220.4 0.0 copy-done.7
  220.4 0.0 copy-done.8
  220.4 0.1 reshape.122
  220.5 0.1 reshape.123
  220.6 0.4 concatenate.12
  221.0 0.2 convolution_convert_fusion.2
  221.3 1.0 copy.47
  222.2 0.0 copy-done.3
  222.2 3.0 %convolution_convert_fusion = bf16[768,2304]{1,0:T(8,128)(2,1)} fusion(bf16[2304,256]{1,0:T(8,128)(2,1)S(1)} %copy-done.3, f32[256,768]{1,0:T(8,128)S(1)} %copy-done.1, f32[768]{0:T(1024)S(1)} %add.31, f32[768]{0:T(1024)S(1)} %mul.102, f32[256]{0:T(256)S(1)} %fusion.5, f32[256]{0:T(256)S(1)} %broadcast_multiply_fusion), kind=kOutput, calls=%fused_computation | convolution fusion | flops 908722176 | bytes 5513216 | tf_op jit(solution)/shard_map/dot_general | solution.py:1273
  225.3 0.0 copy-done.2
  225.3 66.9 %pair_gradient.1 = (f32[96,128]{1,0:T(8,128)}, f32[24,3072]{1,0:T(8,128)}, f32[24,768]{1,0:T(8,128)}, f32[24,2304]{1,0:T(8,128)}, f32[24,256]{1,0:T(8,128)}) custom-call(bf16[4,2048,1024]{2,1,0:T(8,128)(2,1)} %get-tuple-element.73.gs_ref, f32[256,1024]{1,0:T(8,128)} %get-tuple-element.74.dist_ref, bf16[16,128,16384]{2,1,0:T(8,128)(2,1)} %get-tuple-element.75.phi_ref, ...), custom_call_target="tpu_custom_call" | custom-call | tf_op jit(solution)/shard_map/pair_gradient/pallas_call | solution.py:1142
  292.1 2.2 settle_gradients.1
  294.4 1.3 reshape.125
  (16 shorter events, 0.2 us)
Async XLA Ops:
  82.5 4.5 %copy-start = (f32[256,768]{1,0:T(8,128)}, f32[256,768]{1,0:T(8,128)S(1)}, u32[]{:S(2)}) copy-start(f32[256,768]{1,0:T(8,128)S(1)} %get-tuple-element.112.stream_ref) | copy-start | bytes 2359300
  159.0 56.8 %copy-start.1 = (f32[256,768]{1,0:T(8,128)S(1)}, f32[256,768]{1,0:T(8,128)}, u32[]{:S(2)}) copy-start(f32[256,768]{1,0:T(8,128)} %copy-done) | copy-start | bytes 2359300
  215.8 4.2 %copy-start.4 = (f32[256,768]{1,0:T(8,128)S(1)}, f32[256,768]{1,0:T(8,128)}, u32[]{:S(2)}) copy-start(f32[256,768]{1,0:T(8,128)} %get-tuple-element.67) | copy-start | bytes 2359300
  219.6 0.7 copy-start.6
  219.6 0.7 copy-start.5
  219.6 0.7 copy-start.7
  219.6 0.7 copy-start.8
  219.7 2.6 copy-start.3
  220.2 5.1 %copy-start.2 = (f32[256,768]{1,0:T(8,128)}, f32[256,768]{1,0:T(8,128)S(1)}, u32[]{:S(2)}) copy-start(f32[256,768]{1,0:T(8,128)S(1)} %add_add_fusion.1) | copy-start | bytes 2359300

commit v2 on v1

--- a/solution.py
+++ b/solution.py
@@ -25,7 +25,7 @@
 ATT_ROWS = 128
 UNIT_LANES = 768
 UNIT_ROWS = 32
-FEED_LANES = 512
+FEED_LANES = 1024
 SLACK = 2
 LAST_TURNS = 5
 VECTORS = 6
@@ -787,7 +787,7 @@
     place = my_place(sizes)
     block = BlockSum(outbox, near, far, own_ref, near_sems, far_sems, place, sizes)
     if count:
-        opening, turns, closing = stage_turns(scatter_groups(plan, sources, results, scratch, place, sizes))
+        opening, turns, closing = stage_turns(scatter_groups(plan, sources, results, scratch, place, sizes), slack=3)
 
     @pl.when(step == 0)
     def _():

time: 296 us -> 294 us (level)
  no operation moved by 1% of the time
where the time goes in v2:
time: 294 us
  Pallas kernels  271 us (92%)
  matrix products  12.7 us (4%)
  local copies, waits for them, and re-layouts  6.29 us (2%)
  other arithmetic  3.07 us (1%)
    pallas_call x1, Pallas kernels, pair_call(): pl.pallas_call(partial(pair_kernel, sizes, plan, count, steps), grid=(ste...  74.8 us
    pallas_call x1, Pallas kernels, pair_grad_call(): pl.pallas_call(partial(pair_grad_kernel, sizes, plan, count, steps), grid...  66.9 us
    pallas_call x1, Pallas kernels, forward_call(): pl.pallas_call(partial(forward_kernel, sizes, plan, count, parts), grid=(...  55.5 us
    pallas_call x1, Pallas kernels, backward_call(): pl.pallas_call(partial(backward_kernel, sizes, plan, count, GROUPS * part...  55 us
    pallas_call x1, Pallas kernels, feed_call(): pl.pallas_call(partial(feed_kernel, steps), grid=(steps,), in_specs=[in_v...  16.1 us

profile of v2, /device:TPU:0, one launch (start us, length us, event | category | flops | bytes accessed | tf_op | source)
XLA Modules:
  0.0 293.5 jit_solution(12839970887761635050)
XLA Ops:
  0.7 1.2 convert_element_type.27
  1.9 0.7 broadcast_multiply_fusion.1
  2.6 0.3 fusion.3
  2.9 74.8 %pair_bias_and_gather.1 = (f32[256,1024]{1,0:T(8,128)}, bf16[16,128,16384]{2,1,0:T(8,128)(2,1)}, f32[4,2048,1024]{2,1,0:T(8,128)}, bf16[4,2,2,2,32,128]{5,4,3,2,...) custom-call(f32[3,256]{1,0:T(4,128)} %positions.1, ...), custom_call_target="tpu_custom_call" | custom-call | tf_op jit(solution)/shard_map/pair_bias_and_gather/pallas_call | solution.py:487
  77.8 0.8 slice.25
  78.6 0.9 slice.24
  79.6 0.7 broadcast_in_dim_reshape_squeeze.2.bias_in
  80.3 0.7 reshape.116.vectors
  81.0 0.1 mul.102
  81.1 0.1 add.31
  81.1 1.4 fusion.10
  82.5 0.0 copy-start
  82.5 0.2 multiply_reduce_fusion.2
  82.8 4.3 %convolution_convert_fusion.1.q_ref.own_ref = bf16[2304,256]{1,0:T(8,128)(2,1)} fusion(bf16[768,2304]{1,0:T(8,128)(2,1)} %bitcast.73, f32[256,768]{1,0:T(8,128)S(1)} %get-tuple-element.112.stream_ref, f32[768]{0:T(1024)S(1)} %add.31, f32[768]{0:T(1024)S(1)} %mul.102, f32[256]{0:T(256)S(1)} %fusion.5, f32[256]{0:T(256)S(1)} %broadcast_multiply_fusion), kind=kOutput, calls=%fused_computation.1 | convolution fusion | flops 907542528 | bytes 5513216 | tf_op jit(solution)/shard_map/dot_general | solution.py:1249
  87.0 0.0 copy-done
  87.0 55.5 %attention_forward.1 = (bf16[768,256]{1,0:T(8,128)(2,1)}, bf16[4,2048,1024]{2,1,0:T(8,128)(2,1)}, bf16[1536,1024]{1,0:T(8,128)(2,1)}, bf16[4,2,2,2,24,768]{5,4,3...) custom-call(bf16[2304,256]{1,0:T(8,128)(2,1)} %convolution_convert_fusion.1.q_ref.own_ref, ...), custom_call_target="tpu_custom_call" | custom-call | tf_op jit(solution)/shard_map/attention_forward/pallas_call | solution.py:685
  142.5 16.1 %feed_forward.1 = (bf16[256,768]{1,0:T(8,128)(2,1)}, bf16[768,3072]{1,0:T(8,128)(2,1)}, bf16[3072,768]{1,0:T(8,128)(2,1)}, f32[1,3072]{1,0:T(1,128)}, f32[256,76...) custom-call(f32[256,768]{1,0:T(8,128)} %copy-done, ...), custom_call_target="tpu_custom_call" | custom-call | tf_op jit(solution)/shard_map/feed_forward/pallas_call | solution.py:998
  158.7 0.0 copy-start.1
  158.7 55.0 %attention_backward.1 = (bf16[4,2048,1024]{2,1,0:T(8,128)(2,1)}, bf16[2304,256]{1,0:T(8,128)(2,1)}, f32[96,768]{1,0:T(8,128)}) custom-call(bf16[2304,256]{1,0:T(8,128)(2,1)} %convolution_convert_fusion.1.q_ref.own_ref, bf16[768,256]{1,0:T(8,128)(2,1)} %get-tuple-element.68.go_ref, bf16[1536,1024]{1,0:T(8,128)(2,1)} %get-tuple-element.69.k_ref.v_ref, ...), custom_call_target="tpu_custom_call" | custom-call | tf_op jit(solution)/shard_map/attention_backward/pallas_call | solution.py:867
  213.7 0.0 copy-done.1
  213.7 0.0 copy-start.4
  213.7 3.8 %multiply_reduce_fusion = (bf16[768]{0:T(1024)(128)(2,1)S(1)}, f32[256]{0:T(256)S(1)}, bf16[768]{0:T(1024)(128)(2,1)S(1)}, f32[256,768]{1,0:T(8,128)S(1)}) fusion(f32[256,768]{1,0:T(8,128)S(1)} %copy-done.1, f32[256]{0:T(256)S(1)} %fusion.5, f32[256]{0:T(256)S(1)} %broadcast_multiply_fusion, f32[768]{0:T(1024)S(1)} %mul.102, ...), kind=kOutput, calls=%fused_computation.6 | convolution fusion | flops 907540736 | bytes 6300672 | tf_op jit(solution)/shard_map/dot_general | solution.py:1274
  217.4 0.0 copy-start.6
  217.5 0.0 copy-start.5
  217.5 0.0 copy-start.7
  217.5 0.0 copy-start.8
  217.5 0.0 copy-start.3
  217.5 0.3 fusion.8
  217.9 0.0 copy-done.4
  217.9 0.2 add_add_fusion.1
  218.0 0.0 copy-start.2
  218.1 0.1 copy-done.6
  218.1 0.0 copy-done.5
  218.2 0.0 copy-done.7
  218.2 0.0 copy-done.8
  218.2 0.1 reshape.122
  218.4 0.1 reshape.123
  218.5 0.4 concatenate.12
  218.9 0.2 convolution_convert_fusion.2
  219.1 1.0 copy.47
  220.1 0.0 copy-done.3
  220.1 3.0 %convolution_convert_fusion = bf16[768,2304]{1,0:T(8,128)(2,1)} fusion(bf16[2304,256]{1,0:T(8,128)(2,1)S(1)} %copy-done.3, f32[256,768]{1,0:T(8,128)S(1)} %copy-done.1, f32[768]{0:T(1024)S(1)} %add.31, f32[768]{0:T(1024)S(1)} %mul.102, f32[256]{0:T(256)S(1)} %fusion.5, f32[256]{0:T(256)S(1)} %broadcast_multiply_fusion), kind=kOutput, calls=%fused_computation | convolution fusion | flops 908722176 | bytes 5513216 | tf_op jit(solution)/shard_map/dot_general | solution.py:1273
  223.1 0.0 copy-done.2
  223.1 66.9 %pair_gradient.1 = (f32[96,128]{1,0:T(8,128)}, f32[24,3072]{1,0:T(8,128)}, f32[24,768]{1,0:T(8,128)}, f32[24,2304]{1,0:T(8,128)}, f32[24,256]{1,0:T(8,128)}) custom-call(bf16[4,2048,1024]{2,1,0:T(8,128)(2,1)} %get-tuple-element.73.gs_ref, f32[256,1024]{1,0:T(8,128)} %get-tuple-element.74.dist_ref, bf16[16,128,16384]{2,1,0:T(8,128)(2,1)} %get-tuple-element.75.phi_ref, ...), custom_call_target="tpu_custom_call" | custom-call | tf_op jit(solution)/shard_map/pair_gradient/pallas_call | solution.py:1142
  290.0 2.2 settle_gradients.1
  292.2 1.3 reshape.125
  (16 shorter events, 0.2 us)
Async XLA Ops:
  82.5 4.5 %copy-start = (f32[256,768]{1,0:T(8,128)}, f32[256,768]{1,0:T(8,128)S(1)}, u32[]{:S(2)}) copy-start(f32[256,768]{1,0:T(8,128)S(1)} %get-tuple-element.112.stream_ref) | copy-start | bytes 2359300
  158.7 55.0 %copy-start.1 = (f32[256,768]{1,0:T(8,128)S(1)}, f32[256,768]{1,0:T(8,128)}, u32[]{:S(2)}) copy-start(f32[256,768]{1,0:T(8,128)} %copy-done) | copy-start | bytes 2359300
  213.7 4.2 %copy-start.4 = (f32[256,768]{1,0:T(8,128)S(1)}, f32[256,768]{1,0:T(8,128)}, u32[]{:S(2)}) copy-start(f32[256,768]{1,0:T(8,128)} %get-tuple-element.67) | copy-start | bytes 2359300
  217.4 0.7 copy-start.6
  217.5 0.7 copy-start.5
  217.5 0.7 copy-start.7
  217.5 0.7 copy-start.8
  217.5 2.6 copy-start.3
  218.0 5.1 %copy-start.2 = (f32[256,768]{1,0:T(8,128)}, f32[256,768]{1,0:T(8,128)S(1)}, u32[]{:S(2)}) copy-start(f32[256,768]{1,0:T(8,128)S(1)} %add_add_fusion.1) | copy-start | bytes 2359300
